TPU v7x, 512 devices: a whole 4x8x8 slice. The times are simulated.
512 devices in a mesh: grid: 16 (over y, core), tile: 32 (over x, z).
Axes of the slice: x: 4, y: 8, z: 8, core: 2. Of those that a mesh axis runs over, the one named last changes fastest.
Arguments:
- rhs_local: bfloat16 [192, 786432], P(None, ('grid', 'tile')), may hold values from -6 to 6
- diag_inv: bfloat16 [1536, 512, 512], P(('grid', 'tile')), may hold values from -1 to 2, as said below
- codes: bfloat16 [327680, 1536], P(('grid', 'tile')), may hold values from -127 to 127, as said below
- row_scales: float32 [327680], P(('grid', 'tile')), may hold values from 0 to 1, as said below
- sep_index: int32 [327680], P(('grid', 'tile')), may hold values from 0 to 2559, as said below
- live_rows: int32 [512], P(('grid', 'tile')), may hold values from 160 to 640, as said below
- rhs_sep: bfloat16 [192, 2560], P(None, 'tile'), may hold values from -6 to 6
- root_inv: bfloat16 [2560, 2560], P('tile'), may hold values from -1 to 2, as said below
Outputs:
- solution_local: bfloat16 [192, 786432], P(None, ('grid', 'tile'))
- solution_sep: float32 [192, 2560], P(None, 'tile')
Inputs may be any that keep to these rules, and one draw needn't show every extreme that they name: `diag_inv`: each block is upper triangular. `root_inv`: each block is upper triangular. `codes`: Integers. `row_scales`: Positive. `sep_index`: of each device's 640 entries, the j-th run of 20 consecutive entries lies in j * 80 to (j + 1) * 80 - 1, and the entries of one run are distinct. `live_rows`: some device has all 640 rows live.
All inputs are finite; a program needn't handle non-finite values.
Results may differ from a plain program's by a relative error of at most 0.0054.
Values may be sent and summed in bfloat16 or wider, within the bound.
No kernel may reach another device: no remote copies, remote signals or barrier semaphores. Data moves between devices by JAX's collectives and lax.ppermute only.
A program may use at most 64 MiB of HBM per device.

v0:
```python
import jax
import jax.numpy as jnp
from jax import lax
from jax.sharding import PartitionSpec as P


def selector(offsets, share_len):
    columns = jnp.arange(share_len, dtype=jnp.int32)
    return (offsets[:, :, None] == columns[None, None, :]).astype(jnp.float32)


def on_device(rhs_local, diag_inv, codes, row_scales, sep_index, live_rows, rhs_sep, root_inv):
    rhs_count, local_len = rhs_local.shape
    per_dev, block_len = (diag_inv.shape[0], diag_inv.shape[1])
    coupled_rows = codes.shape[0]
    share_len, sep_len = root_inv.shape
    tile_count = lax.axis_size("tile")
    per_share = coupled_rows // tile_count
    pieces = []
    for block_pos in range(per_dev):
        columns = rhs_local[:, block_pos * block_len : (block_pos + 1) * block_len]
        pieces.append(jnp.dot(columns, diag_inv[block_pos], preferred_element_type=jnp.float32))
    forward_flat = jnp.concatenate(pieces, axis=1).astype(jnp.bfloat16)
    positions = jnp.arange(coupled_rows, dtype=jnp.int32)
    row_factor = row_scales * (positions < live_rows[0]).astype(jnp.float32)
    coupled = (
        lax.dot_general(
            forward_flat, codes, (((1,), (1,)), ((), ())), preferred_element_type=jnp.float32
        )
        * row_factor[None, :]
    )
    bases = (jnp.arange(tile_count, dtype=jnp.int32) * share_len)[:, None]
    local_offsets = sep_index.reshape(tile_count, per_share) - bases
    onehot = selector(local_offsets, share_len)
    values = coupled.reshape(rhs_count, tile_count, per_share)
    partial_value = jnp.einsum(
        "rjp,jps->rjs", values, onehot, precision=lax.Precision.HIGHEST
    ).reshape(rhs_count, sep_len)
    summed = lax.psum(partial_value, ("grid", "tile"))
    own_share = lax.dynamic_slice_in_dim(summed, lax.axis_index("tile") * share_len, share_len, 1)
    residue = (rhs_sep.astype(jnp.float32) - own_share).astype(jnp.bfloat16)
    root_part = jnp.dot(residue, root_inv, preferred_element_type=jnp.float32)
    forward_sep = lax.psum(root_part, "tile").astype(jnp.bfloat16)
    solved = lax.dot_general(
        forward_sep, root_inv, (((1,), (1,)), ((), ())), preferred_element_type=jnp.float32
    )
    gathered = lax.all_gather(solved.astype(jnp.bfloat16), "tile", axis=1, tiled=True)
    gathered_split = gathered.astype(jnp.float32).reshape(rhs_count, tile_count, share_len)
    picked = jnp.einsum(
        "rjs,jps->rjp", gathered_split, onehot, precision=lax.Precision.HIGHEST
    ).reshape(rhs_count, coupled_rows)
    weighted = (picked * row_factor[None, :]).astype(jnp.bfloat16)
    update = jnp.dot(weighted, codes, preferred_element_type=jnp.float32)
    misfit = (forward_flat.astype(jnp.float32) - update).astype(jnp.bfloat16)
    results = []
    for block_pos in range(per_dev):
        columns = misfit[:, block_pos * block_len : (block_pos + 1) * block_len]
        results.append(
            lax.dot_general(
                columns,
                diag_inv[block_pos],
                (((1,), (1,)), ((), ())),
                preferred_element_type=jnp.float32,
            )
        )
    result = jnp.concatenate(results, axis=1)
    return (result.astype(jnp.bfloat16), solved)


def solution(mesh):
    return jax.shard_map(
        on_device,
        mesh=mesh,
        in_specs=(
            P(None, ("grid", "tile")),
            P(("grid", "tile"), None, None),
            P(("grid", "tile"), None),
            P(("grid", "tile")),
            P(("grid", "tile")),
            P(("grid", "tile")),
            P(None, "tile"),
            P("tile", None),
        ),
        out_specs=(P(None, ("grid", "tile")), P(None, "tile")),
        check_vma=False,
    )
```

profile of v0, /device:TPU:34, one launch (start us, length us, event | category | flops | bytes accessed | tf_op | source)
XLA Modules:
  0.0 530.7 jit_solution(14506760942146203309)
XLA Ops:
  7.2 0.0 all-reduce.3.cloned.1.call-start
  7.2 1.5 convolution_convert_fusion.3
  8.8 1.5 convolution_convert_fusion.4
  10.3 1.5 convolution_convert_fusion.5
  12.5 0.8 convolution_multiply_fusion
  13.3 0.2 copy.12
  13.6 0.1 reshape.44
  13.6 0.4 copy-done.3
  14.0 0.1 reshape.43
  14.1 0.1 broadcast_subtract_fusion
  14.2 3.0 fusion.15
  17.2 285.0 %all-reduce.3.cloned.1.call-done = f32[192,2560]{0,1:T(8,128)} async-done(((f32[192,2560]{0,1:T(8,128)}), f32[192,2560]{0,1:T(8,128)}) %all-reduce.3.cloned.1.call-update) | async-done | bytes 1966096 | tf_op jit(solution)/shard_map/psum | solution.py:39
  302.2 2.6 fusion.25
  304.8 154.0 %all-reduce.4 = bf16[192,2560]{1,0:T(8,128)(2,1)S(1)} all-reduce(f32[192,2560]{1,0:T(8,128)} %fusion.25), channel_id=1, replica_groups=mesh['grid'=16,'tile'=32] {'tile'}, use_global_device_ids=true, to_apply=%region_1.0 | all-reduce | flops 491520 | bytes 2949120 | tf_op jit(solution)/shard_map/psum | solution.py:43
  458.8 1.1 fusion.29
  459.8 59.6 %all_gather.3 = bf16[192,2560]{0,1:T(8,128)(2,1)S(1)} all-gather(bf16[192,80]{0,1:T(8,128)(2,1)S(1)} %get-tuple-element.2), channel_id=1, replica_groups=mesh['grid'=16,'tile'=32] {'tile'}, dimensions={1}, use_global_device_ids=true | all-gather | bytes 1013760 | tf_op jit(solution)/shard_map/all_gather | solution.py:47
  519.5 0.4 convolution_bitcast_fusion
  519.8 0.1 reshape.47
  519.9 0.2 copy.13
  520.1 1.9 fusion
  522.0 0.3 convolution_convert_fusion
  522.4 0.3 convolution_convert_fusion.1
  522.7 0.3 convolution_convert_fusion.2
  523.0 0.9 pad_maximum_fusion.1
  (20 shorter events, 0.1 us)
Async XLA Ops:
  7.2 5.3 %copy-start = (bf16[640,1536]{1,0:T(8,128)(2,1)S(1)}, bf16[640,1536]{1,0:T(8,128)(2,1)}, u32[]{:S(2)}) copy-start(bf16[640,1536]{1,0:T(8,128)(2,1)} %param.10) | copy-start | bytes 5898244
  7.2 5.3 copy-start.4
  7.2 295.0 %all-reduce.3.cloned.1.call-start = ((), (), s32[]{:S(2)}) async-start(), calls=%async_computation | async-start | bytes 5242880 | tf_op jit(solution)/shard_map/psum | solution.py:39
  8.8 3.7 copy-start.6
  10.3 2.2 copy-start.7
  11.8 0.7 copy-start.8
  13.3 0.7 copy-start.3
  17.1 285.0 %copy-start.1 = (bf16[80,2560]{1,0:T(8,128)(2,1)S(1)}, bf16[80,2560]{1,0:T(8,128)(2,1)}, u32[]{:S(2)}) copy-start(bf16[80,2560]{1,0:T(8,128)(2,1)} %param.15) | copy-start | bytes 1228804
  17.1 285.0 %copy-start.2 = (bf16[192,80]{0,1:T(8,128)(2,1)S(1)}, bf16[192,80]{0,1:T(8,128)(2,1)}, u32[]{:S(2)}) copy-start(bf16[192,80]{0,1:T(8,128)(2,1)} %param.14) | copy-start | bytes 92164
  520.1 1.9 copy-start.5
Sparse Core Ops, SparseCore 0:
  17.3 284.8 all-reduce.2
where the time goes:
time: 531 us
  waiting for transfers between devices  285 us (54%)
  blocking collectives  214 us (40%)
  matrix products  15.1 us (3%)
  between operations  14.9 us (3%)
    psum x1, waiting for transfers between devices, on_device(): summed = lax.psum(partial_value, ('grid', 'tile'))  285 us
    psum x1, blocking collectives, on_device(): forward_sep = lax.psum(root_part, 'tile').astype(jnp.bfloat16)  154 us
    all_gather x1, blocking collectives, on_device(): lax.all_gather(solved.astype(jnp.bfloat16), 'tile', axis=1, tiled=True)  59.6 us
  transfers between devices with their start and end apart: 1, of which 1 were waited for; matrix products, arithmetic and copies ran while one was open for 0% of the time, Pallas kernels for 0%

commit v1 on v0

v1 whole, which is shorter than its diff:
```python
import jax
import jax.numpy as jnp
from jax import lax
from jax.sharding import PartitionSpec as P

LANES = 128


def round_up(value, step):
    return -(-value // step) * step


def on_device(rhs_local, diag_inv, codes, row_scales, sep_index, live_rows, rhs_sep, root_inv):
    rhs_count, local_len = rhs_local.shape
    per_dev, block_len = (diag_inv.shape[0], diag_inv.shape[1])
    coupled_rows = codes.shape[0]
    share_len, sep_len = root_inv.shape
    tile_count = lax.axis_size("tile")
    grid_count = lax.axis_size("grid")
    per_share = coupled_rows // tile_count
    chunk_rows = round_up(per_share, 8)
    own_rhs = rhs_count // grid_count
    value_lanes = round_up(rhs_count + 1, LANES)
    share_lanes = round_up(share_len, LANES)

    pieces = []
    for block_pos in range(per_dev):
        columns = rhs_local[:, block_pos * block_len : (block_pos + 1) * block_len]
        pieces.append(jnp.dot(columns, diag_inv[block_pos], preferred_element_type=jnp.float32))
    forward_flat = jnp.concatenate(pieces, axis=1).astype(jnp.bfloat16)
    positions = jnp.arange(coupled_rows, dtype=jnp.int32)
    row_factor = row_scales * (positions < live_rows[0]).astype(jnp.float32)
    coupled = (
        lax.dot_general(
            codes, forward_flat, (((1,), (1,)), ((), ())), preferred_element_type=jnp.float32
        )
        * row_factor[:, None]
    )
    offsets = (sep_index - positions // per_share * share_len).astype(jnp.float32)
    payload = jnp.concatenate(
        [
            coupled,
            offsets[:, None],
            jnp.zeros((coupled_rows, value_lanes - rhs_count - 1), jnp.float32),
        ],
        axis=1,
    )
    payload = payload.reshape(tile_count, per_share, value_lanes)
    payload = jnp.pad(payload, ((0, 0), (0, chunk_rows - per_share), (0, 0))).astype(jnp.bfloat16)
    arrived = lax.all_to_all(payload, "tile", 0, 0, tiled=True)
    arrived = arrived.reshape(tile_count * chunk_rows, value_lanes)
    columns = jnp.arange(share_lanes, dtype=jnp.int32).astype(jnp.bfloat16)
    onehot = (arrived[:, rhs_count : rhs_count + 1] == columns[None, :]).astype(jnp.bfloat16)
    partial_value = lax.dot_general(
        arrived[:, :rhs_count],
        onehot,
        (((0,), (0,)), ((), ())),
        preferred_element_type=jnp.float32,
    )
    partial_value = partial_value.reshape(grid_count, own_rhs, share_lanes)
    own_share = lax.all_to_all(partial_value, "grid", 0, 0, tiled=True).sum(axis=0)
    own_right = lax.dynamic_slice_in_dim(rhs_sep, lax.axis_index("grid") * own_rhs, own_rhs, 0)
    residue = (own_right.astype(jnp.float32) - own_share[:, :share_len]).astype(jnp.bfloat16)
    spaced = root_inv.reshape(share_len, tile_count, share_len)
    spaced = jnp.pad(spaced, ((0, 0), (0, 0), (0, share_lanes - share_len)))
    spaced = spaced.reshape(share_len, tile_count * share_lanes)
    root_part = jnp.dot(residue, spaced, preferred_element_type=jnp.float32)
    root_part = root_part.reshape(own_rhs, tile_count, share_lanes).transpose(1, 0, 2)
    forward_sep = lax.all_to_all(root_part, "tile", 0, 0, tiled=True).sum(axis=0)
    forward_sep = jnp.broadcast_to(
        forward_sep.astype(jnp.bfloat16)[None], (tile_count, own_rhs, share_lanes)
    )
    forward_sep = lax.all_to_all(forward_sep, "tile", 0, 0, tiled=True)
    forward_sep = forward_sep.transpose(1, 0, 2).reshape(own_rhs, tile_count * share_lanes)
    solved = lax.dot_general(
        forward_sep, spaced, (((1,), (1,)), ((), ())), preferred_element_type=jnp.float32
    )
    solved = jnp.broadcast_to(solved[None], (grid_count, own_rhs, share_len))
    solved = lax.all_to_all(solved, "grid", 0, 0, tiled=True).reshape(rhs_count, share_len)
    picked = lax.dot_general(
        onehot[:, :share_len],
        solved.astype(jnp.bfloat16),
        (((1,), (1,)), ((), ())),
        preferred_element_type=jnp.float32,
    ).astype(jnp.bfloat16)
    picked = picked.reshape(tile_count, chunk_rows, rhs_count)
    picked = lax.all_to_all(picked, "tile", 0, 0, tiled=True)
    picked = picked[:, :per_share].reshape(coupled_rows, rhs_count)
    weighted = (picked.astype(jnp.float32) * row_factor[:, None]).astype(jnp.bfloat16)
    update = lax.dot_general(
        weighted, codes, (((0,), (0,)), ((), ())), preferred_element_type=jnp.float32
    )
    misfit = (forward_flat.astype(jnp.float32) - update).astype(jnp.bfloat16)
    results = []
    for block_pos in range(per_dev):
        columns = misfit[:, block_pos * block_len : (block_pos + 1) * block_len]
        results.append(
            lax.dot_general(
                columns,
                diag_inv[block_pos],
                (((1,), (1,)), ((), ())),
                preferred_element_type=jnp.float32,
            )
        )
    result = jnp.concatenate(results, axis=1)
    return (result.astype(jnp.bfloat16), solved)


def solution(mesh):
    return jax.shard_map(
        on_device,
        mesh=mesh,
        in_specs=(
            P(None, ("grid", "tile")),
            P(("grid", "tile"), None, None),
            P(("grid", "tile"), None),
            P(("grid", "tile")),
            P(("grid", "tile")),
            P(("grid", "tile")),
            P(None, "tile"),
            P("tile", None),
        ),
        out_specs=(P(None, ("grid", "tile")), P(None, "tile")),
        check_vma=False,
    )
```

time: 531 us -> 125 us (0.24)
  the two profiles are of different devices: /device:TPU:34 before, /device:TPU:64 now
where the time goes in v1:
time: 125 us; the launch traced here: 124 us
  waiting for transfers between devices  43.7 us (35%)
  blocking collectives  31.9 us (26%)
  starting transfers between devices  27.5 us (22%)
  matrix products  9.33 us (7%)
  local copies, waits for them, and re-layouts  7.72 us (6%)
  other arithmetic  2.13 us (2%)
  between operations  1.63 us (1%)
    all_to_all x1, blocking collectives, on_device(): lax.all_to_all(root_part, 'tile', 0, 0, tiled=True).sum(axis=0)  17.5 us
    all_to_all x1, waiting for transfers between devices, on_device(): arrived = lax.all_to_all(payload, 'tile', 0, 0, tiled=True)  14.9 us
    all_to_all x1, waiting for transfers between devices, on_device(): picked = lax.all_to_all(picked, 'tile', 0, 0, tiled=True)  14.9 us
    all_to_all x1, blocking collectives, on_device(): forward_sep = lax.all_to_all(forward_sep, 'tile', 0, 0, tiled=True)  14.3 us
    all_to_all x1, starting transfers between devices, on_device(): arrived = lax.all_to_all(payload, 'tile', 0, 0, tiled=True)  12.6 us
    all_to_all x1, waiting for transfers between devices, on_device(): lax.all_to_all(solved, 'grid', 0, 0, tiled=True)  7.59 us
    all_to_all x1, starting transfers between devices, on_device(): lax.all_to_all(partial_value, 'grid', 0, 0, tiled=True).sum(axis=0)  7.2 us
    all_to_all x1, waiting for transfers between devices, on_device(): lax.all_to_all(partial_value, 'grid', 0, 0, tiled=True).sum(axis=0)  6.41 us
  transfers between devices with their start and end apart: 4, of which 4 were waited for; matrix products, arithmetic and copies ran while one was open for 3% of the time, Pallas kernels for 0%

profile of v1, /device:TPU:64, one launch (start us, length us, event | category | flops | bytes accessed | tf_op | source)
XLA Modules:
  0.0 123.9 jit_solution(16044223538919256180)
XLA Ops:
  0.7 1.5 %convolution_convert_fusion.6 = bf16[192,512]{1,0:T(8,128)(2,1)S(1)} fusion(bf16[3,512,512]{2,1,0:T(8,128)(2,1)} %param.9, bf16[192,1536]{1,0:T(8,128)(2,1)} %param.8), kind=kOutput, calls=%fused_computation.10 | convolution fusion | flops 100761600 | bytes 917504 | tf_op jit(solution)/shard_map/dot_general | solution.py:29
  2.2 1.5 %convolution_convert_fusion.4 = bf16[192,512]{1,0:T(8,128)(2,1)S(1)} fusion(bf16[3,512,512]{2,1,0:T(8,128)(2,1)} %param.9, bf16[192,1536]{1,0:T(8,128)(2,1)} %param.8), kind=kOutput, calls=%fused_computation.8 | convolution fusion | flops 100761600 | bytes 917504 | tf_op jit(solution)/shard_map/dot_general | solution.py:29
  3.7 1.5 %convolution_convert_fusion.5 = bf16[192,512]{1,0:T(8,128)(2,1)S(1)} fusion(bf16[3,512,512]{2,1,0:T(8,128)(2,1)} %param.9, bf16[192,1536]{1,0:T(8,128)(2,1)} %param.8), kind=kOutput, calls=%fused_computation.9 | convolution fusion | flops 100761600 | bytes 917504 | tf_op jit(solution)/shard_map/dot_general | solution.py:29
  6.2 0.8 fusion.2
  7.5 0.8 pad.9
  8.3 12.6 %all-to-all-start = ((bf16[32,24,256]{2,1,0:T(8,128)(2,1)}), bf16[32,24,256]{2,1,0:T(8,128)(2,1)S(1)}, u32[]{:S(2)}, u32[]{:S(2)}) async-start(bf16[32,24,256]{2,1,0:T(8,128)(2,1)} %pad.9), calls=%async_computation | async-start | bytes 786432 | tf_op jit(solution)/shard_map/all_to_all | solution.py:50
  20.9 14.9 %all-to-all-done = bf16[32,24,256]{2,1,0:T(8,128)(2,1)S(1)} async-done(((bf16[32,24,256]{2,1,0:T(8,128)(2,1)}), bf16[32,24,256]{2,1,0:T(8,128)(2,1)S(1)}, u32[]{:S(2)}, u32[]{:S(2)}) %all-to-all-start) | async-done | bytes 393248 | tf_op jit(solution)/shard_map/all_to_all | solution.py:50
  36.4 0.7 reshape.45
  37.1 7.2 %all-to-all-start.1 = ((f32[16,12,128]{2,1,0:T(8,128)}), f32[16,12,128]{2,1,0:T(8,128)S(1)}, u32[]{:S(2)}, u32[]{:S(2)}) async-start(f32[16,12,128]{2,1,0:T(8,128)} %reshape.45), calls=%async_computation.1 | async-start | bytes 262144 | tf_op jit(solution)/shard_map/all_to_all | solution.py:61
  44.5 1.8 %reshape.46 = bf16[80,32,80]{2,1,0:T(8,128)(2,1)S(1)} reshape(bf16[80,2560]{1,0:T(8,128)(2,1)} %param.15) | data formatting | bytes 819200 | tf_op jit(solution)/shard_map/reshape | solution.py:64
  46.5 6.4 %all-to-all-done.1 = f32[16,12,128]{2,1,0:T(8,128)S(1)} async-done(((f32[16,12,128]{2,1,0:T(8,128)}), f32[16,12,128]{2,1,0:T(8,128)S(1)}, u32[]{:S(2)}, u32[]{:S(2)}) %all-to-all-start.1) | async-done | bytes 98336 | tf_op jit(solution)/shard_map/all_to_all | solution.py:61
  53.2 17.5 %all_to_all.30 = f32[32,12,128]{2,1,0:T(8,128)S(1)} all-to-all(f32[32,12,128]{2,1,0:T(8,128)S(1)} %convolution_bitcast_fusion), channel_id=1, replica_groups=mesh['grid'=16,'tile'=32] {'tile'}, dimensions={0} | all-to-all | bytes 393216 | tf_op jit(solution)/shard_map/all_to_all | solution.py:69
  70.8 14.3 %all_to_all.31 = bf16[32,12,128]{2,1,0:T(8,128)(2,1)S(1)} all-to-all(bf16[32,12,128]{2,1,0:T(8,128)(2,1)S(1)} %broadcast_in_dim.7), channel_id=1, replica_groups=mesh['grid'=16,'tile'=32] {'tile'}, dimensions={0} | all-to-all | bytes 196608 | tf_op jit(solution)/shard_map/all_to_all | solution.py:73
  85.4 0.8 reshape.54
  86.2 3.5 %all-to-all-start.4 = ((f32[16,1,960]{2,1,0:T(1,128)}), f32[16,1,960]{2,1,0:T(1,128)S(1)}, u32[]{:S(2)}, u32[]{:S(2)}) async-start(f32[16,1,960]{2,1,0:T(1,128)} %reshape.54), calls=%async_computation.4 | async-start | bytes 131072 | tf_op jit(solution)/shard_map/all_to_all | solution.py:79
  89.9 7.6 %all-to-all-done.4 = f32[16,1,960]{2,1,0:T(1,128)S(1)} async-done(((f32[16,1,960]{2,1,0:T(1,128)}), f32[16,1,960]{2,1,0:T(1,128)S(1)}, u32[]{:S(2)}, u32[]{:S(2)}) %all-to-all-start.4) | async-done | bytes 61472 | tf_op jit(solution)/shard_map/all_to_all | solution.py:79
  97.5 0.5 broadcast.20
  98.0 0.8 reduce.2
  99.2 0.9 copy.38
  100.1 4.2 %all-to-all-start.5 = ((bf16[32,24,192]{2,1,0:T(8,128)(2,1)}), bf16[32,24,192]{2,1,0:T(8,128)(2,1)S(1)}, u32[]{:S(2)}, u32[]{:S(2)}) async-start(bf16[32,24,192]{2,1,0:T(8,128)(2,1)} %bitcast.11), calls=%async_computation.5 | async-start | bytes 786432 | tf_op jit(solution)/shard_map/all_to_all | solution.py:87
  104.4 0.7 copy.39
  105.1 14.9 %all-to-all-done.5 = bf16[32,24,192]{2,1,0:T(8,128)(2,1)S(1)} async-done(((bf16[32,24,192]{2,1,0:T(8,128)(2,1)}), bf16[32,24,192]{2,1,0:T(8,128)(2,1)S(1)}, u32[]{:S(2)}, u32[]{:S(2)}) %all-to-all-start.5) | async-done | bytes 294944 | tf_op jit(solution)/shard_map/all_to_all | solution.py:87
  120.1 2.0 %fusion = bf16[192,1536]{1,0:T(8,128)(2,1)S(1)} fusion(bf16[640,1536]{1,0:T(8,128)(2,1)S(1)} %copy-done, f32[640,192]{1,0:T(8,128)S(1)} %reshape.50, f32[640]{0:T(1024)S(1)} %fusion.42, bf16[192,512]{1,0:T(8,128)(2,1)} %copy-done.6, bf16[192,512]{1,0:T(8,128)(2,1)} %copy-done.7, bf16[192,512]{1,0:T(8,128)(2,1)} %copy-done.5), kind=kOutput, calls=%fused_computation.1 | convolution fusion | flops 380092416 | bytes 3639808 | tf_op jit(solution)/shard_map/dot_general | solution.py:90
  123.1 0.9 pad_maximum_fusion.1
  (45 shorter events, 4.1 us)
Async XLA Ops:
  0.6 5.6 %copy-start = (bf16[640,1536]{1,0:T(8,128)(2,1)S(1)}, bf16[640,1536]{1,0:T(8,128)(2,1)}, u32[]{:S(2)}) copy-start(bf16[640,1536]{1,0:T(8,128)(2,1)} %param.10) | copy-start | bytes 5898244
  0.6 5.2 %copy-start.2 = (s32[640]{0:T(1024)S(1)}, s32[640]{0:T(1024)}, u32[]{:S(2)}) copy-start(s32[640]{0:T(1024)} %param.12) | copy-start | bytes 7684
  0.7 5.5 %copy-start.3 = (f32[640]{0:T(1024)S(1)}, f32[640]{0:T(1024)}, u32[]{:S(2)}) copy-start(f32[640]{0:T(1024)} %param.11) | copy-start | bytes 7684
  2.2 4.0 %copy-start.5 = (bf16[192,512]{1,0:T(8,128)(2,1)}, bf16[192,512]{1,0:T(8,128)(2,1)S(1)}, u32[]{:S(2)}) copy-start(bf16[192,512]{1,0:T(8,128)(2,1)S(1)} %convolution_convert_fusion.6) | copy-start | bytes 589828
  3.7 2.5 %copy-start.6 = (bf16[192,512]{1,0:T(8,128)(2,1)}, bf16[192,512]{1,0:T(8,128)(2,1)S(1)}, u32[]{:S(2)}) copy-start(bf16[192,512]{1,0:T(8,128)(2,1)S(1)} %convolution_convert_fusion.4) | copy-start | bytes 589828
  5.2 31.9 %copy-start.7 = (bf16[192,512]{1,0:T(8,128)(2,1)}, bf16[192,512]{1,0:T(8,128)(2,1)S(1)}, u32[]{:S(2)}) copy-start(bf16[192,512]{1,0:T(8,128)(2,1)S(1)} %convolution_convert_fusion.5) | copy-start | bytes 589828
  7.5 36.8 %copy-start.1 = (bf16[192,80]{0,1:T(8,128)(2,1)S(1)}, bf16[192,80]{0,1:T(8,128)(2,1)}, u32[]{:S(2)}) copy-start(bf16[192,80]{0,1:T(8,128)(2,1)} %param.14) | copy-start | bytes 92164
  8.3 27.5 %all-to-all-start = ((bf16[32,24,256]{2,1,0:T(8,128)(2,1)}), bf16[32,24,256]{2,1,0:T(8,128)(2,1)S(1)}, u32[]{:S(2)}, u32[]{:S(2)}) async-start(bf16[32,24,256]{2,1,0:T(8,128)(2,1)} %pad.9), calls=%async_computation | async-start | bytes 786432 | tf_op jit(solution)/shard_map/all_to_all | solution.py:50
  37.1 15.9 %all-to-all-start.1 = ((f32[16,12,128]{2,1,0:T(8,128)}), f32[16,12,128]{2,1,0:T(8,128)S(1)}, u32[]{:S(2)}, u32[]{:S(2)}) async-start(f32[16,12,128]{2,1,0:T(8,128)} %reshape.45), calls=%async_computation.1 | async-start | bytes 262144 | tf_op jit(solution)/shard_map/all_to_all | solution.py:61
  86.2 11.3 %all-to-all-start.4 = ((f32[16,1,960]{2,1,0:T(1,128)}), f32[16,1,960]{2,1,0:T(1,128)S(1)}, u32[]{:S(2)}, u32[]{:S(2)}) async-start(f32[16,1,960]{2,1,0:T(1,128)} %reshape.54), calls=%async_computation.4 | async-start | bytes 131072 | tf_op jit(solution)/shard_map/all_to_all | solution.py:79
  100.1 19.8 %all-to-all-start.5 = ((bf16[32,24,192]{2,1,0:T(8,128)(2,1)}), bf16[32,24,192]{2,1,0:T(8,128)(2,1)S(1)}, u32[]{:S(2)}, u32[]{:S(2)}) async-start(bf16[32,24,192]{2,1,0:T(8,128)(2,1)} %bitcast.11), calls=%async_computation.5 | async-start | bytes 786432 | tf_op jit(solution)/shard_map/all_to_all | solution.py:87
  120.1 2.0 %copy-start.4 = (bf16[3,512,512]{2,1,0:T(8,128)(2,1)S(1)}, bf16[3,512,512]{2,1,0:T(8,128)(2,1)}, u32[]{:S(2)}) copy-start(bf16[3,512,512]{2,1,0:T(8,128)(2,1)} %param.9) | copy-start | bytes 4718596

commit v2 on v0

v2 whole, which is shorter than its diff:
```python
import functools

import jax
import jax.numpy as jnp
from jax import lax
from jax.experimental import pallas as pl
from jax.experimental.pallas import tpu as pltpu
from jax.sharding import PartitionSpec as P

LANES = 128
HALF = 64
F32 = jnp.float32
BF16 = jnp.bfloat16
VMEM_BYTES = 24 * 1024 * 1024
ANY = pl.BlockSpec(memory_space=pl.ANY)
VMEM = pl.BlockSpec(memory_space=pltpu.VMEM)
SMEM = pl.BlockSpec(memory_space=pltpu.SMEM)


def round_up(value, step):
    return -(-value // step) * step


def factor_columns(scales_ref, live_ref):
    groups = scales_ref.shape[0]
    row = lax.broadcasted_iota(jnp.int32, (groups, LANES), 0)
    lane = lax.broadcasted_iota(jnp.int32, (groups, LANES), 1)
    live = (row * LANES + lane) < live_ref[0]
    factors = scales_ref[...] * live.astype(F32)
    if groups < LANES:
        factors = jnp.concatenate([factors, jnp.zeros((LANES - groups, LANES), F32)], axis=0)
    return factors.T


def dot(left, right, left_dim=1, right_dim=0):
    return lax.dot_general(
        left, right, (((left_dim,), (right_dim,)), ((), ())), preferred_element_type=F32
    )


def forward_kernel(
    per_share, rhs_hbm, diag_hbm, codes_hbm, scales_ref, offsets_ref, live_ref,
    forward_ref, chunks_ref,
    rhs, diag, codes, coupled, packed, sems,
):
    blocks, block_len = diag.shape[0], diag.shape[1]
    rows, rhs_count = codes.shape[0], rhs.shape[0]
    half = per_share // 2
    copies = [pltpu.make_async_copy(rhs_hbm, rhs, sems.at[0])]
    for block in range(blocks):
        copies.append(
            pltpu.make_async_copy(diag_hbm.at[block], diag.at[block], sems.at[1 + block])
        )
    copies.append(pltpu.make_async_copy(codes_hbm, codes, sems.at[1 + blocks]))
    for copy in copies:
        copy.start()
    factors = factor_columns(scales_ref, live_ref)
    packed[...] = jnp.zeros_like(packed)
    copies[0].wait()
    for block in range(blocks):
        copies[1 + block].wait()
        columns = slice(block * block_len, (block + 1) * block_len)
        forward_ref[:, columns] = dot(rhs[:, columns], diag[block]).astype(BF16)
    copies[-1].wait()
    for group in range(0, rows, LANES):
        span = slice(group, min(group + LANES, rows))
        count = span.stop - span.start
        value = dot(codes[span, :], forward_ref[...], 1, 1)
        value = value * factors[:count, group // LANES : group // LANES + 1]
        coupled[span, :LANES] = value[:, :LANES]
        tail = value[:, LANES:]
        coupled[span, LANES : LANES + HALF] = tail
        coupled[span, LANES + HALF :] = tail
    low_lane = lax.broadcasted_iota(jnp.int32, (half, LANES), 1) < HALF
    for peer in range(rows // per_share):
        first = peer * per_share
        packed[peer, :per_share, :] = coupled[first : first + per_share, :LANES]
        packed[peer, per_share : per_share + half, :] = jnp.where(
            low_lane,
            coupled[first : first + half, LANES:],
            coupled[first + half : first + per_share, LANES:],
        )
        packed[peer, per_share + half : per_share + half + 1, :] = offsets_ref[peer : peer + 1, :]
    chunks_ref[...] = packed[...].astype(BF16)


def sum_kernel(per_share, chunks_ref, hot_ref, sums_ref, wide, table, total):
    peers, chunk_rows = chunks_ref.shape[0], chunks_ref.shape[1]
    members, own_pad = sums_ref.shape[0], sums_ref.shape[1]
    half = per_share // 2
    wide[...] = chunks_ref[...].astype(F32)
    for peer in range(peers):
        table[peer : peer + 1, :] = wide[peer, per_share + half : per_share + half + 1, :]
    if peers < LANES:
        table[peers:, :] = jnp.zeros((LANES - peers, LANES), F32)
    offsets = table[...].T
    row = lax.broadcasted_iota(jnp.int32, (LANES, LANES), 0)
    tail_row = jnp.logical_and(row >= per_share, row < per_share + half)
    shifts = (
        jnp.where(row < per_share, offsets, -1.0),
        jnp.where(tail_row, pltpu.roll(offsets, per_share, 0), -1.0),
        jnp.where(tail_row, pltpu.roll(offsets, half, 0), -1.0),
    )
    lane = lax.broadcasted_iota(jnp.int32, (chunk_rows, LANES), 1).astype(F32)
    for peer in range(peers):
        span = slice(peer * chunk_rows, (peer + 1) * chunk_rows)
        for part, shifted in enumerate(shifts):
            hit = shifted[:chunk_rows, peer : peer + 1] == lane
            hot_ref[span, part * LANES : (part + 1) * LANES] = hit.astype(F32).astype(BF16)
    values = wide[...].reshape(peers * chunk_rows, LANES).T.astype(BF16)
    result = dot(values, hot_ref[...])
    total[:LANES, :] = result[:, :LANES]
    total[LANES:, :] = result[:HALF, LANES : 2 * LANES] + result[HALF:, 2 * LANES :]
    own = total.shape[0] // members
    if own < own_pad:
        sums_ref[...] = jnp.zeros_like(sums_ref)
    for member in range(members):
        sums_ref[member, :own, :] = total[member * own : (member + 1) * own, :].astype(BF16)


def spread_kernel(own, solved_ref, solution_ref, picker_ref, wide, total):
    members = solved_ref.shape[0]
    wide[...] = solved_ref[...].astype(F32)
    for member in range(members):
        total[member * own : (member + 1) * own, :] = wide[member, :own, :]
    value = total[...]
    tail = value[LANES:, :].astype(BF16)
    nothing = jnp.zeros((HALF, LANES), BF16)
    picker_ref[:, :LANES] = value[:LANES, :].astype(BF16)
    picker_ref[:HALF, LANES : 2 * LANES] = tail
    picker_ref[HALF:, LANES : 2 * LANES] = nothing
    picker_ref[:HALF, 2 * LANES :] = nothing
    picker_ref[HALF:, 2 * LANES :] = tail
    padded = jnp.concatenate([value, jnp.zeros((HALF, LANES), F32)], axis=0)
    flipped = padded.T
    solution_ref[...] = flipped[: solution_ref.shape[0], : solution_ref.shape[1]]


def backward_kernel(
    per_share, chunks_ref, scales_ref, live_ref, forward_ref, codes_hbm, diag_hbm,
    result_ref,
    codes, diag, wide, picked, sems,
):
    blocks, block_len = diag.shape[0], diag.shape[1]
    rows, rhs_count = codes.shape[0], forward_ref.shape[0]
    half = per_share // 2
    copies = [pltpu.make_async_copy(codes_hbm, codes, sems.at[0])]
    for block in range(blocks):
        copies.append(
            pltpu.make_async_copy(diag_hbm.at[block], diag.at[block], sems.at[1 + block])
        )
    for copy in copies:
        copy.start()
    factors = factor_columns(scales_ref, live_ref)
    wide[...] = chunks_ref[...].astype(F32)
    for peer in range(rows // per_share):
        first = peer * per_share
        picked[first : first + per_share, :LANES] = wide[peer, :per_share, :]
        tail = wide[peer, per_share : per_share + half, :]
        picked[first : first + half, LANES:] = tail
        picked[first + half : first + per_share, LANES:] = pltpu.roll(tail, HALF, 1)
    weighted = []
    for group in range(0, rows, LANES):
        span = slice(group, min(group + LANES, rows))
        count = span.stop - span.start
        value = picked[span, :] * factors[:count, group // LANES : group // LANES + 1]
        weighted.append(value.T[:rhs_count].astype(BF16))
    weighted = jnp.concatenate(weighted, axis=1)
    copies[0].wait()
    for block in range(blocks):
        columns = slice(block * block_len, (block + 1) * block_len)
        update = dot(weighted, codes[:, columns])
        misfit = (forward_ref[:, columns].astype(F32) - update).astype(BF16)
        copies[1 + block].wait()
        result_ref[:, columns] = dot(misfit, diag[block], 1, 1).astype(BF16)


def params():
    return pltpu.CompilerParams(vmem_limit_bytes=VMEM_BYTES)


def cost(flops, moved):
    return pl.CostEstimate(flops=flops, bytes_accessed=moved, transcendentals=0)


def on_device(rhs_local, diag_inv, codes, row_scales, sep_index, live_rows, rhs_sep, root_inv):
    rhs_count, local_len = rhs_local.shape
    per_dev, block_len = (diag_inv.shape[0], diag_inv.shape[1])
    coupled_rows = codes.shape[0]
    share_len, sep_len = root_inv.shape
    tile_count = lax.axis_size("tile")
    grid_count = lax.axis_size("grid")
    per_share = coupled_rows // tile_count
    chunk_rows = round_up(per_share + per_share // 2 + 1, 16)
    own_rhs = rhs_count // grid_count
    own_pad = round_up(own_rhs, 16)

    groups = -(-coupled_rows // LANES)
    scales = jnp.pad(row_scales, (0, groups * LANES - coupled_rows)).reshape(groups, LANES)
    starts = jnp.arange(tile_count, dtype=jnp.int32)[:, None] * share_len
    offsets = (sep_index.reshape(tile_count, per_share) - starts).astype(F32)
    offsets = jnp.pad(offsets, ((0, 0), (0, LANES - per_share)))

    forward_flat, chunks = pl.pallas_call(
        functools.partial(forward_kernel, per_share),
        out_shape=(
            jax.ShapeDtypeStruct((rhs_count, local_len), BF16),
            jax.ShapeDtypeStruct((tile_count, chunk_rows, LANES), BF16),
        ),
        in_specs=[ANY, ANY, ANY, VMEM, VMEM, SMEM],
        out_specs=(VMEM, VMEM),
        scratch_shapes=[
            pltpu.VMEM((rhs_count, local_len), BF16),
            pltpu.VMEM(diag_inv.shape, BF16),
            pltpu.VMEM(codes.shape, BF16),
            pltpu.VMEM((coupled_rows, 2 * LANES), F32),
            pltpu.VMEM((tile_count, chunk_rows, LANES), F32),
            pltpu.SemaphoreType.DMA((2 + per_dev,)),
        ],
        compiler_params=params(),
        cost_estimate=cost(2 * rhs_count * local_len * (block_len + coupled_rows), 5 << 20),
        name="forward",
    )(rhs_local, diag_inv, codes, scales, offsets, live_rows)
    arrived = lax.all_to_all(chunks, "tile", 0, 0, tiled=True)
    onehot, sums = pl.pallas_call(
        functools.partial(sum_kernel, per_share),
        out_shape=(
            jax.ShapeDtypeStruct((tile_count * chunk_rows, 3 * LANES), BF16),
            jax.ShapeDtypeStruct((grid_count, own_pad, LANES), BF16),
        ),
        in_specs=[VMEM],
        out_specs=(VMEM, VMEM),
        scratch_shapes=[
            pltpu.VMEM((tile_count, chunk_rows, LANES), F32),
            pltpu.VMEM((LANES, LANES), F32),
            pltpu.VMEM((rhs_count, LANES), F32),
        ],
        compiler_params=params(),
        cost_estimate=cost(2 * tile_count * chunk_rows * 3 * LANES * LANES, 1 << 20),
        name="gather_sum",
    )(arrived)
    own_share = lax.all_to_all(sums, "grid", 0, 0, tiled=True).astype(F32).sum(axis=0)
    own_right = lax.dynamic_slice_in_dim(rhs_sep, lax.axis_index("grid") * own_rhs, own_rhs, 0)
    own_right = jnp.pad(own_right, ((0, own_pad - own_rhs), (0, LANES - share_len)))
    residue = (own_right.astype(F32) - own_share)[:, :share_len].astype(BF16)
    spaced = root_inv.reshape(share_len, tile_count, share_len)
    spaced = jnp.pad(spaced, ((0, 0), (0, 0), (0, LANES - share_len)))
    spaced = spaced.reshape(share_len, tile_count * LANES)
    root_part = jnp.dot(residue, spaced, preferred_element_type=F32).astype(BF16)
    root_part = root_part.reshape(own_pad, tile_count, LANES).transpose(1, 0, 2)
    forward_sep = lax.all_to_all(root_part, "tile", 0, 0, tiled=True).astype(F32).sum(axis=0)
    forward_sep = jnp.broadcast_to(
        forward_sep.astype(BF16)[None], (tile_count, own_pad, LANES)
    )
    forward_sep = lax.all_to_all(forward_sep, "tile", 0, 0, tiled=True)
    forward_sep = forward_sep.transpose(1, 0, 2).reshape(own_pad, tile_count * LANES)
    solved = dot(forward_sep, spaced, 1, 1)
    solved = jnp.pad(solved.astype(BF16), ((0, 0), (0, LANES - share_len)))
    solved = jnp.broadcast_to(solved[None], (grid_count, own_pad, LANES))
    solved = lax.all_to_all(solved, "grid", 0, 0, tiled=True)
    solution_sep, picker = pl.pallas_call(
        functools.partial(spread_kernel, own_rhs),
        out_shape=(
            jax.ShapeDtypeStruct((share_len, rhs_count), F32),
            jax.ShapeDtypeStruct((LANES, 3 * LANES), BF16),
        ),
        in_specs=[VMEM],
        out_specs=(VMEM, VMEM),
        scratch_shapes=[
            pltpu.VMEM((grid_count, own_pad, LANES), F32),
            pltpu.VMEM((rhs_count, LANES), F32),
        ],
        compiler_params=params(),
        name="spread",
    )(solved)
    picked = dot(onehot, picker, 1, 1).astype(BF16)
    picked = picked.reshape(tile_count, chunk_rows, LANES)
    picked = lax.all_to_all(picked, "tile", 0, 0, tiled=True)
    result = pl.pallas_call(
        functools.partial(backward_kernel, per_share),
        out_shape=jax.ShapeDtypeStruct((rhs_count, local_len), BF16),
        in_specs=[VMEM, VMEM, SMEM, VMEM, ANY, ANY],
        out_specs=VMEM,
        scratch_shapes=[
            pltpu.VMEM(codes.shape, BF16),
            pltpu.VMEM(diag_inv.shape, BF16),
            pltpu.VMEM((tile_count, chunk_rows, LANES), F32),
            pltpu.VMEM((coupled_rows, 2 * LANES), F32),
            pltpu.SemaphoreType.DMA((1 + per_dev,)),
        ],
        compiler_params=params(),
        cost_estimate=cost(2 * rhs_count * local_len * (block_len + coupled_rows), 5 << 20),
        name="backward",
    )(picked, scales, live_rows, forward_flat, codes, diag_inv)
    return (result, solution_sep.T)


def solution(mesh):
    return jax.shard_map(
        on_device,
        mesh=mesh,
        in_specs=(
            P(None, ("grid", "tile")),
            P(("grid", "tile"), None, None),
            P(("grid", "tile"), None),
            P(("grid", "tile")),
            P(("grid", "tile")),
            P(("grid", "tile")),
            P(None, "tile"),
            P("tile", None),
        ),
        out_specs=(P(None, ("grid", "tile")), P(None, "tile")),
        check_vma=False,
    )
```

time: 531 us -> 114 us (0.21)
  the two profiles are of different devices: /device:TPU:34 before, /device:TPU:64 now
where the time goes in v2:
time: 114 us; the launch traced here: 113 us
  blocking collectives  80.7 us (71%)
  Pallas kernels  8.56 us (8%)
  starting transfers between devices  7.2 us (6%)
  local copies, waits for them, and re-layouts  6.87 us (6%)
  waiting for transfers between devices  6.5 us (6%)
  matrix products  1.9 us (2%)
  between operations  1.45 us (1%)
    all_to_all x1, blocking collectives, on_device(): arrived = lax.all_to_all(chunks, 'tile', 0, 0, tiled=True)  24.7 us
    all_to_all x1, blocking collectives, on_device(): picked = lax.all_to_all(picked, 'tile', 0, 0, tiled=True)  17 us
    all_to_all x1, blocking collectives, on_device(): lax.all_to_all(root_part, 'tile', 0, 0, tiled=True).astype(F32).sum(axis=0)  14.8 us
    all_to_all x1, blocking collectives, on_device(): forward_sep = lax.all_to_all(forward_sep, 'tile', 0, 0, tiled=True)  13.9 us
    all_to_all x1, blocking collectives, on_device(): solved = lax.all_to_all(solved, 'grid', 0, 0, tiled=True)  10.4 us
    all_to_all x1, starting transfers between devices, on_device(): lax.all_to_all(sums, 'grid', 0, 0, tiled=True).astype(F32).sum(axis=0)  7.2 us
    all_to_all x1, waiting for transfers between devices, on_device(): lax.all_to_all(sums, 'grid', 0, 0, tiled=True).astype(F32).sum(axis=0)  6.5 us
    unnamed x21, local copies, waits for them, and re-layouts  4.81 us
  transfers between devices with their start and end apart: 1, of which 1 were waited for; matrix products, arithmetic and copies ran while one was open for 1% of the time, Pallas kernels for 0%

profile of v2, /device:TPU:64, one launch (start us, length us, event | category | flops | bytes accessed | tf_op | source)
XLA Modules:
  0.0 113.3 jit_solution(2402429883566003032)
XLA Ops:
  1.3 0.8 reshape.31
  2.1 0.1 subtract_convert_fusion
  2.2 1.5 %copy-done.1 = bf16[640,1536]{1,0:T(8,128)(2,1)S(1)} copy-done((bf16[640,1536]{1,0:T(8,128)(2,1)S(1)}, bf16[640,1536]{1,0:T(8,128)(2,1)}, u32[]{:S(2)}) %copy-start.1) | copy-done | bytes 1966104
  3.7 1.4 %copy-done.3 = bf16[3,512,512]{2,1,0:T(8,128)(2,1)S(1)} copy-done((bf16[3,512,512]{2,1,0:T(8,128)(2,1)S(1)}, bf16[3,512,512]{2,1,0:T(8,128)(2,1)}, u32[]{:S(2)}) %copy-start.3) | copy-done | bytes 1572888
  5.1 1.1 copy-done.5
  6.2 0.7 copy-done.6
  6.9 3.0 %forward.1 = (bf16[192,1536]{1,0:T(8,128)(2,1)S(1)}, bf16[32,32,128]{2,1,0:T(8,128)(2,1)S(1)}) custom-call(bf16[192,1536]{1,0:T(8,128)(2,1)S(1)} %copy-done.5, bf16[3,512,512]{2,1,0:T(8,128)(2,1)S(1)} %copy-done.3, bf16[640,1536]{1,0:T(8,128)(2,1)S(1)} %copy-done.1, f32[5,128]{1,0:T(8,128)S(1)} %bitcast.27, f32[32,128]{1,0:T(8,128)S(1)} %pad.16.offsets_ref, ...), custom_call_target="tpu_custom_call" | custom-call | flops 679477248 | bytes 5242880 | tf_op jit(solution)/shard_map/forward/pallas_call | solution.py:204
  9.9 24.7 %all_to_all.30.chunks_ref = bf16[32,32,128]{2,1,0:T(8,128)(2,1)S(1)} all-to-all(bf16[32,32,128]{2,1,0:T(8,128)(2,1)S(1)} %get-tuple-element.8), channel_id=1, replica_groups=mesh['grid'=16,'tile'=32] {'tile'}, dimensions={0} | all-to-all | bytes 524288 | tf_op jit(solution)/shard_map/all_to_all | solution.py:224
  34.6 1.4 %gather_sum.1 = (bf16[1024,384]{1,0:T(8,128)(2,1)S(1)}, bf16[16,16,128]{2,1,0:T(8,128)(2,1)}) custom-call(bf16[32,32,128]{2,1,0:T(8,128)(2,1)S(1)} %all_to_all.30.chunks_ref), custom_call_target="tpu_custom_call" | custom-call | flops 100663296 | bytes 1048576 | tf_op jit(solution)/shard_map/gather_sum/pallas_call | solution.py:225
  36.0 7.2 %all-to-all-start.1 = ((bf16[16,16,128]{2,1,0:T(8,128)(2,1)}), bf16[16,16,128]{2,1,0:T(8,128)(2,1)S(1)}, u32[]{:S(2)}, u32[]{:S(2)}) async-start(bf16[16,16,128]{2,1,0:T(8,128)(2,1)} %get-tuple-element.10), calls=%async_computation.1 | async-start | bytes 131072 | tf_op jit(solution)/shard_map/all_to_all | solution.py:242
  43.3 0.1 constant_dynamic-slice_fusion
  43.3 0.1 copy.16
  43.4 0.8 reshape.32
  44.3 0.3 copy.13
  44.5 6.5 %all-to-all-done.1 = bf16[16,16,128]{2,1,0:T(8,128)(2,1)S(1)} async-done(((bf16[16,16,128]{2,1,0:T(8,128)(2,1)}), bf16[16,16,128]{2,1,0:T(8,128)(2,1)S(1)}, u32[]{:S(2)}, u32[]{:S(2)}) %all-to-all-start.1) | async-done | bytes 65568 | tf_op jit(solution)/shard_map/all_to_all | solution.py:242
  51.1 0.2 fusion
  51.3 14.8 %all_to_all.31 = bf16[32,16,128]{2,1,0:T(8,128)(2,1)S(1)} all-to-all(bf16[32,16,128]{2,1,0:T(8,128)(2,1)S(1)} %bitcast.30), channel_id=1, replica_groups=mesh['grid'=16,'tile'=32] {'tile'}, dimensions={0} | all-to-all | bytes 262144 | tf_op jit(solution)/shard_map/all_to_all | solution.py:251
  66.2 13.9 %all_to_all.32 = bf16[32,16,128]{2,1,0:T(8,128)(2,1)S(1)} all-to-all(bf16[32,16,128]{2,1,0:T(8,128)(2,1)S(1)} %broadcast_in_dim.4), channel_id=1, replica_groups=mesh['grid'=16,'tile'=32] {'tile'}, dimensions={0} | all-to-all | bytes 262144 | tf_op jit(solution)/shard_map/all_to_all | solution.py:255
  80.1 1.3 %fusion.1 = bf16[16,80]{1,0:T(8,128)(2,1)S(1)} fusion(bf16[80,32,80]{2,0,1:T(8,128)(2,1)} %copy-done.8, bf16[32,16,128]{2,1,0:T(8,128)(2,1)S(1)} %all_to_all.32), kind=kOutput, calls=%fused_computation.4 | convolution fusion | flops 10487040 | bytes 543232 | tf_op jit(solution)/shard_map/dot_general | solution.py:36
  81.5 10.4 %all_to_all.33.solved_ref = bf16[16,16,128]{2,1,0:T(8,128)(2,1)S(1)} all-to-all(bf16[16,16,128]{2,1,0:T(8,128)(2,1)S(1)} %broadcast_in_dim.5), channel_id=1, replica_groups=mesh['grid'=16,'tile'=32] {'grid'}, dimensions={0} | all-to-all | bytes 131072 | tf_op jit(solution)/shard_map/all_to_all | solution.py:260
  91.9 0.7 spread.1
  92.6 0.4 convolution_convert_fusion.1
  93.0 17.0 %all_to_all.34.chunks_ref = bf16[32,32,128]{2,1,0:T(8,128)(2,1)S(1)} all-to-all(bf16[32,32,128]{2,1,0:T(8,128)(2,1)S(1)} %bitcast.29), channel_id=1, replica_groups=mesh['grid'=16,'tile'=32] {'tile'}, dimensions={0} | all-to-all | bytes 524288 | tf_op jit(solution)/shard_map/all_to_all | solution.py:278
  110.0 3.4 %backward.1 = bf16[192,1536]{1,0:T(8,128)(2,1)} custom-call(bf16[32,32,128]{2,1,0:T(8,128)(2,1)S(1)} %all_to_all.34.chunks_ref, f32[5,128]{1,0:T(8,128)S(1)} %bitcast.28, s32[1]{0:T(128)S(6)} %copy.25.live_ref, bf16[192,1536]{1,0:T(8,128)(2,1)S(1)} %get-tuple-element.12.forward_ref, bf16[640,1536]{1,0:T(8,128)(2,1)S(1)} %copy-done.2, ...), custom_call_target="tpu_custom_call" | custom-call | flops 679477248 | bytes 5242880 | tf_op jit(solution)/shard_map/backward/pallas_call | solution.py:279
  (24 shorter events, 0.2 us)
Async XLA Ops:
  0.6 42.6 %copy-start = (bf16[192,80]{0,1:T(8,128)(2,1)S(1)}, bf16[192,80]{0,1:T(8,128)(2,1)}, u32[]{:S(2)}) copy-start(bf16[192,80]{0,1:T(8,128)(2,1)} %param.14) | copy-start | bytes 92164
  2.2 1.6 %copy-start.1 = (bf16[640,1536]{1,0:T(8,128)(2,1)S(1)}, bf16[640,1536]{1,0:T(8,128)(2,1)}, u32[]{:S(2)}) copy-start(bf16[640,1536]{1,0:T(8,128)(2,1)} %codes_hbm.3) | copy-start | bytes 5898244
  3.7 1.4 %copy-start.3 = (bf16[3,512,512]{2,1,0:T(8,128)(2,1)S(1)}, bf16[3,512,512]{2,1,0:T(8,128)(2,1)}, u32[]{:S(2)}) copy-start(bf16[3,512,512]{2,1,0:T(8,128)(2,1)} %diag_hbm.3) | copy-start | bytes 4718596
  5.1 1.1 copy-start.5
  6.2 0.7 copy-start.6
  6.9 36.5 %copy-start.9 = (bf16[80,2560]{1,0:T(8,128)(2,1)S(1)}, bf16[80,2560]{1,0:T(8,128)(2,1)}, u32[]{:S(2)}) copy-start(bf16[80,2560]{1,0:T(8,128)(2,1)} %param.15) | copy-start | bytes 1228804
  36.0 15.0 %all-to-all-start.1 = ((bf16[16,16,128]{2,1,0:T(8,128)(2,1)}), bf16[16,16,128]{2,1,0:T(8,128)(2,1)S(1)}, u32[]{:S(2)}, u32[]{:S(2)}) async-start(bf16[16,16,128]{2,1,0:T(8,128)(2,1)} %get-tuple-element.10), calls=%async_computation.1 | async-start | bytes 131072 | tf_op jit(solution)/shard_map/all_to_all | solution.py:242
  44.5 6.5 %copy-start.8 = (bf16[80,32,80]{2,0,1:T(8,128)(2,1)}, bf16[80,32,80]{2,0,1:T(8,128)(2,1)S(1)}, u32[]{:S(2)}) copy-start(bf16[80,32,80]{2,0,1:T(8,128)(2,1)S(1)} %copy.13) | copy-start | bytes 1228804
  51.3 58.7 %copy-start.2 = (bf16[640,1536]{1,0:T(8,128)(2,1)S(1)}, bf16[640,1536]{1,0:T(8,128)(2,1)}, u32[]{:S(2)}) copy-start(bf16[640,1536]{1,0:T(8,128)(2,1)} %codes_hbm.3) | copy-start | bytes 5898244
  51.3 58.7 %copy-start.7 = (f32[640]{0:T(1024)S(1)}, f32[640]{0:T(1024)}, u32[]{:S(2)}) copy-start(f32[640]{0:T(1024)} %param.11) | copy-start | bytes 7684
  66.1 43.8 %copy-start.4 = (bf16[3,512,512]{2,1,0:T(8,128)(2,1)S(1)}, bf16[3,512,512]{2,1,0:T(8,128)(2,1)}, u32[]{:S(2)}) copy-start(bf16[3,512,512]{2,1,0:T(8,128)(2,1)} %diag_hbm.3) | copy-start | bytes 4718596

commit v3 on v2

--- a/solution.py
+++ b/solution.py
@@ -11,10 +11,12 @@
 HALF = 64
 F32 = jnp.float32
 BF16 = jnp.bfloat16
-VMEM_BYTES = 24 * 1024 * 1024
+MIB = 1024 * 1024
+ALL_VMEM = 67043328
 ANY = pl.BlockSpec(memory_space=pl.ANY)
 VMEM = pl.BlockSpec(memory_space=pltpu.VMEM)
 SMEM = pl.BlockSpec(memory_space=pltpu.SMEM)
+HBM = pl.BlockSpec(memory_space=pltpu.HBM)
 
 
 def round_up(value, step):
@@ -38,8 +40,29 @@
     )
 
 
+def offset_rows(index_ref, peers, per_share, share_len):
+    groups = index_ref.shape[0]
+    table = index_ref[...].astype(F32)
+    if groups < LANES:
+        table = jnp.concatenate([table, jnp.zeros((LANES - groups, LANES), F32)], axis=0)
+    table = table.T
+    row = lax.broadcasted_iota(jnp.int32, (LANES, LANES), 0).astype(F32)
+    lane = lax.broadcasted_iota(jnp.int32, (LANES, LANES), 1).astype(F32)
+    peer_row = lax.broadcasted_iota(jnp.int32, (peers, LANES), 0).astype(F32)
+    peer_lane = lax.broadcasted_iota(jnp.int32, (peers, LANES), 1).astype(F32)
+    total = jnp.zeros((peers, LANES), F32)
+    for group in range(groups):
+        peer = jnp.floor((row + (group * LANES + 0.5)) * (1.0 / per_share))
+        place = row + group * LANES - peer * per_share
+        spread = jnp.where(place == lane, table[:, group : group + 1] - peer * share_len, 0.0)
+        owner = jnp.floor((peer_lane + (group * LANES + 0.5)) * (1.0 / per_share))
+        chosen = (owner == peer_row).astype(F32)
+        total = total + dot(chosen.astype(BF16), spread.astype(BF16))
+    return total
+
+
 def forward_kernel(
-    per_share, rhs_hbm, diag_hbm, codes_hbm, scales_ref, offsets_ref, live_ref,
+    per_share, share_len, rhs_hbm, diag_hbm, codes_hbm, scales_ref, index_ref, live_ref,
     forward_ref, chunks_ref,
     rhs, diag, codes, coupled, packed, sems,
 ):
@@ -55,6 +78,7 @@
     for copy in copies:
         copy.start()
     factors = factor_columns(scales_ref, live_ref)
+    offsets = offset_rows(index_ref, rows // per_share, per_share, share_len)
     packed[...] = jnp.zeros_like(packed)
     copies[0].wait()
     for block in range(blocks):
@@ -80,7 +104,7 @@
             coupled[first : first + half, LANES:],
             coupled[first + half : first + per_share, LANES:],
         )
-        packed[peer, per_share + half : per_share + half + 1, :] = offsets_ref[peer : peer + 1, :]
+        packed[peer, per_share + half : per_share + half + 1, :] = offsets[peer : peer + 1, :]
     chunks_ref[...] = packed[...].astype(BF16)
 
 
@@ -175,8 +199,8 @@
         result_ref[:, columns] = dot(misfit, diag[block], 1, 1).astype(BF16)
 
 
-def params():
-    return pltpu.CompilerParams(vmem_limit_bytes=VMEM_BYTES)
+def params(limit):
+    return pltpu.CompilerParams(vmem_limit_bytes=limit)
 
 
 def cost(flops, moved):
@@ -197,17 +221,15 @@
 
     groups = -(-coupled_rows // LANES)
     scales = jnp.pad(row_scales, (0, groups * LANES - coupled_rows)).reshape(groups, LANES)
-    starts = jnp.arange(tile_count, dtype=jnp.int32)[:, None] * share_len
-    offsets = (sep_index.reshape(tile_count, per_share) - starts).astype(F32)
-    offsets = jnp.pad(offsets, ((0, 0), (0, LANES - per_share)))
+    indices = jnp.pad(sep_index, (0, groups * LANES - coupled_rows)).reshape(groups, LANES)
 
     forward_flat, chunks = pl.pallas_call(
-        functools.partial(forward_kernel, per_share),
+        functools.partial(forward_kernel, per_share, share_len),
         out_shape=(
             jax.ShapeDtypeStruct((rhs_count, local_len), BF16),
             jax.ShapeDtypeStruct((tile_count, chunk_rows, LANES), BF16),
         ),
-        in_specs=[ANY, ANY, ANY, VMEM, VMEM, SMEM],
+        in_specs=[HBM, HBM, HBM, VMEM, VMEM, SMEM],
         out_specs=(VMEM, VMEM),
         scratch_shapes=[
             pltpu.VMEM((rhs_count, local_len), BF16),
@@ -217,10 +239,10 @@
             pltpu.VMEM((tile_count, chunk_rows, LANES), F32),
             pltpu.SemaphoreType.DMA((2 + per_dev,)),
         ],
-        compiler_params=params(),
+        compiler_params=params(ALL_VMEM),
         cost_estimate=cost(2 * rhs_count * local_len * (block_len + coupled_rows), 5 << 20),
         name="forward",
-    )(rhs_local, diag_inv, codes, scales, offsets, live_rows)
+    )(rhs_local, diag_inv, codes, scales, indices, live_rows)
     arrived = lax.all_to_all(chunks, "tile", 0, 0, tiled=True)
     onehot, sums = pl.pallas_call(
         functools.partial(sum_kernel, per_share),
@@ -235,7 +257,7 @@
             pltpu.VMEM((LANES, LANES), F32),
             pltpu.VMEM((rhs_count, LANES), F32),
         ],
-        compiler_params=params(),
+        compiler_params=params(8 * MIB),
         cost_estimate=cost(2 * tile_count * chunk_rows * 3 * LANES * LANES, 1 << 20),
         name="gather_sum",
     )(arrived)
@@ -270,7 +292,7 @@
             pltpu.VMEM((grid_count, own_pad, LANES), F32),
             pltpu.VMEM((rhs_count, LANES), F32),
         ],
-        compiler_params=params(),
+        compiler_params=params(4 * MIB),
         name="spread",
     )(solved)
     picked = dot(onehot, picker, 1, 1).astype(BF16)
@@ -288,7 +310,7 @@
             pltpu.VMEM((coupled_rows, 2 * LANES), F32),
             pltpu.SemaphoreType.DMA((1 + per_dev,)),
         ],
-        compiler_params=params(),
+        compiler_params=params(16 * MIB),
         cost_estimate=cost(2 * rhs_count * local_len * (block_len + coupled_rows), 5 << 20),
         name="backward",
     )(picked, scales, live_rows, forward_flat, codes, diag_inv)

time: 114 us -> 115 us (level)
  Pallas kernels: 8.56 us -> 10.6 us
  local copies, waits for them, and re-layouts: 6.87 us -> 5.05 us
  waiting for transfers between devices: 6.5 us -> 4.78 us
    unnamed x21 -> x13, local copies, waits for them, and re-layouts: 4.81 us -> 2.05 us
    pallas_call x1, Pallas kernels: 3.02 us -> 5.04 us  [on_device(): pl.pallas_call(functools.partial(forward_kernel, per_share, share_len), o...]
    all_to_all x1, waiting for transfers between devices: 6.5 us -> 4.78 us  [on_device(): lax.all_to_all(sums, 'grid', 0, 0, tiled=True).astype(F32).sum(axis=0)]
  transfers between devices with their start and end apart: 1 -> 1, of which waited for: 1 -> 1; matrix products, arithmetic and copies ran while one was open for 1% -> 3% of each run, Pallas kernels for 0% -> 0%
where the time goes in v3:
time: 115 us; the launch traced here: 114 us
  blocking collectives  81.2 us (71%)
  Pallas kernels  10.6 us (9%)
  starting transfers between devices  7.2 us (6%)
  local copies, waits for them, and re-layouts  5.05 us (4%)
  waiting for transfers between devices  4.78 us (4%)
  matrix products  3.04 us (3%)
  between operations  1.41 us (1%)
    all_to_all x1, blocking collectives, on_device(): arrived = lax.all_to_all(chunks, 'tile', 0, 0, tiled=True)  24.9 us
    all_to_all x1, blocking collectives, on_device(): picked = lax.all_to_all(picked, 'tile', 0, 0, tiled=True)  16.9 us
    all_to_all x1, blocking collectives, on_device(): lax.all_to_all(root_part, 'tile', 0, 0, tiled=True).astype(F32).sum(axis=0)  15 us
    all_to_all x1, blocking collectives, on_device(): forward_sep = lax.all_to_all(forward_sep, 'tile', 0, 0, tiled=True)  13.8 us
    all_to_all x1, blocking collectives, on_device(): solved = lax.all_to_all(solved, 'grid', 0, 0, tiled=True)  10.6 us
    all_to_all x1, starting transfers between devices, on_device(): lax.all_to_all(sums, 'grid', 0, 0, tiled=True).astype(F32).sum(axis=0)  7.2 us
    pallas_call x1, Pallas kernels, on_device(): pl.pallas_call(functools.partial(forward_kernel, per_share, share_len), o...  5.04 us
    all_to_all x1, waiting for transfers between devices, on_device(): lax.all_to_all(sums, 'grid', 0, 0, tiled=True).astype(F32).sum(axis=0)  4.78 us
  transfers between devices with their start and end apart: 1, of which 1 were waited for; matrix products, arithmetic and copies ran while one was open for 3% of the time, Pallas kernels for 0%

profile of v3, /device:TPU:64, one launch (start us, length us, event | category | flops | bytes accessed | tf_op | source)
XLA Modules:
  0.0 114.2 jit_solution(12652086680394059144)
XLA Ops:
  1.3 5.0 %forward.1 = (bf16[192,1536]{1,0:T(8,128)(2,1)}, bf16[32,32,128]{2,1,0:T(8,128)(2,1)}) custom-call(bf16[192,1536]{1,0:T(8,128)(2,1)} %rhs_hbm.1, bf16[3,512,512]{2,1,0:T(8,128)(2,1)} %diag_hbm.3, bf16[640,1536]{1,0:T(8,128)(2,1)} %codes_hbm.3, f32[5,128]{1,0:T(8,128)} %bitcast.28, s32[5,128]{1,0:T(8,128)} %bitcast.32, s32[1]{0:T(128)S(6)} %copy.25.live_ref), custom_call_target="tpu_custom_call" | custom-call | flops 679477248 | bytes 5242880 | tf_op jit(solution)/shard_map/forward/pallas_call | solution.py:226
  6.3 24.9 %all_to_all.30.chunks_ref = bf16[32,32,128]{2,1,0:T(8,128)(2,1)S(1)} all-to-all(bf16[32,32,128]{2,1,0:T(8,128)(2,1)} %get-tuple-element.8), channel_id=1, replica_groups=mesh['grid'=16,'tile'=32] {'tile'}, dimensions={0} | all-to-all | bytes 524288 | tf_op jit(solution)/shard_map/all_to_all | solution.py:246
  31.2 1.4 %gather_sum.1 = (bf16[1024,384]{1,0:T(8,128)(2,1)S(1)}, bf16[16,16,128]{2,1,0:T(8,128)(2,1)}) custom-call(bf16[32,32,128]{2,1,0:T(8,128)(2,1)S(1)} %all_to_all.30.chunks_ref), custom_call_target="tpu_custom_call" | custom-call | flops 100663296 | bytes 1048576 | tf_op jit(solution)/shard_map/gather_sum/pallas_call | solution.py:247
  32.6 0.9 copy-done.2
  33.5 7.2 %all-to-all-start.1 = ((bf16[16,16,128]{2,1,0:T(8,128)(2,1)}), bf16[16,16,128]{2,1,0:T(8,128)(2,1)S(1)}, u32[]{:S(2)}, u32[]{:S(2)}) async-start(bf16[16,16,128]{2,1,0:T(8,128)(2,1)} %get-tuple-element.10), calls=%async_computation.1 | async-start | bytes 131072 | tf_op jit(solution)/shard_map/all_to_all | solution.py:264
  40.7 0.9 constant_dynamic-slice_fusion
  41.6 0.1 copy.16
  41.7 1.8 %reshape.27 = bf16[80,32,80]{2,1,0:T(8,128)(2,1)S(1)} reshape(bf16[80,2560]{1,0:T(8,128)(2,1)} %param.15) | data formatting | bytes 819200 | tf_op jit(solution)/shard_map/reshape | solution.py:268
  43.5 0.3 copy.13
  43.7 4.8 %all-to-all-done.1 = bf16[16,16,128]{2,1,0:T(8,128)(2,1)S(1)} async-done(((bf16[16,16,128]{2,1,0:T(8,128)(2,1)}), bf16[16,16,128]{2,1,0:T(8,128)(2,1)S(1)}, u32[]{:S(2)}, u32[]{:S(2)}) %all-to-all-start.1) | async-done | bytes 65568 | tf_op jit(solution)/shard_map/all_to_all | solution.py:264
  48.6 0.2 fusion
  48.8 0.0 copy-start
  48.8 0.0 copy-start.4
  48.8 15.0 %all_to_all.31 = bf16[32,16,128]{2,1,0:T(8,128)(2,1)} all-to-all(bf16[32,16,128]{2,1,0:T(8,128)(2,1)S(1)} %bitcast.31), channel_id=1, replica_groups=mesh['grid'=16,'tile'=32] {'tile'}, dimensions={0} | all-to-all | bytes 262144 | tf_op jit(solution)/shard_map/all_to_all | solution.py:273
  63.8 0.9 reduce_sum.22
  64.8 13.8 %all_to_all.32 = bf16[32,16,128]{2,1,0:T(8,128)(2,1)S(1)} all-to-all(bf16[32,16,128]{2,1,0:T(8,128)(2,1)S(1)} %broadcast_in_dim.4), channel_id=1, replica_groups=mesh['grid'=16,'tile'=32] {'tile'}, dimensions={0} | all-to-all | bytes 262144 | tf_op jit(solution)/shard_map/all_to_all | solution.py:277
  78.6 1.3 %fusion.1 = bf16[16,80]{1,0:T(8,128)(2,1)S(1)} fusion(bf16[80,32,80]{2,0,1:T(8,128)(2,1)} %copy-done.5, bf16[32,16,128]{2,1,0:T(8,128)(2,1)S(1)} %all_to_all.32), kind=kOutput, calls=%fused_computation.4 | convolution fusion | flops 10487040 | bytes 543232 | tf_op jit(solution)/shard_map/dot_general | solution.py:38
  80.0 10.6 %all_to_all.33.solved_ref = bf16[16,16,128]{2,1,0:T(8,128)(2,1)S(1)} all-to-all(bf16[16,16,128]{2,1,0:T(8,128)(2,1)S(1)} %broadcast_in_dim.5), channel_id=1, replica_groups=mesh['grid'=16,'tile'=32] {'grid'}, dimensions={0} | all-to-all | bytes 131072 | tf_op jit(solution)/shard_map/all_to_all | solution.py:282
  90.6 0.7 spread.1
  91.4 1.5 %convolution_convert_fusion.1 = bf16[1024,128]{1,0:T(8,128)(2,1)S(1)} fusion(bf16[1024,384]{1,0:T(8,128)(2,1)} %copy-done.2, bf16[128,384]{1,0:T(8,128)(2,1)S(1)} %get-tuple-element.11), kind=kOutput, calls=%fused_computation.1 | convolution fusion | flops 100794368 | bytes 1146880 | tf_op jit(solution)/shard_map/dot_general | solution.py:38
  92.9 16.9 %all_to_all.34.chunks_ref = bf16[32,32,128]{2,1,0:T(8,128)(2,1)S(1)} all-to-all(bf16[32,32,128]{2,1,0:T(8,128)(2,1)S(1)} %bitcast.30), channel_id=1, replica_groups=mesh['grid'=16,'tile'=32] {'tile'}, dimensions={0} | all-to-all | bytes 524288 | tf_op jit(solution)/shard_map/all_to_all | solution.py:300
  109.8 0.0 copy-start.3
  109.8 1.1 copy-done.3
  110.9 3.3 %backward.1 = bf16[192,1536]{1,0:T(8,128)(2,1)} custom-call(bf16[32,32,128]{2,1,0:T(8,128)(2,1)S(1)} %all_to_all.34.chunks_ref, f32[5,128]{1,0:T(8,128)S(1)} %bitcast.29, s32[1]{0:T(128)S(6)} %copy.25.live_ref, bf16[192,1536]{1,0:T(8,128)(2,1)S(1)} %copy-done.3, bf16[640,1536]{1,0:T(8,128)(2,1)S(1)} %copy-done, bf16[3,512,512]{2,1,0:T(8,128)(2,1)S(1)} %copy-done.1), custom_call_target="tpu_custom_call" | custom-call | flops 679477248 | bytes 5242880 | tf_op jit(solution)/shard_map/backward/pallas_call | solution.py:301
  (12 shorter events, 0.1 us)
Async XLA Ops:
  32.6 0.9 copy-start.2
  33.5 15.0 %all-to-all-start.1 = ((bf16[16,16,128]{2,1,0:T(8,128)(2,1)}), bf16[16,16,128]{2,1,0:T(8,128)(2,1)S(1)}, u32[]{:S(2)}, u32[]{:S(2)}) async-start(bf16[16,16,128]{2,1,0:T(8,128)(2,1)} %get-tuple-element.10), calls=%async_computation.1 | async-start | bytes 131072 | tf_op jit(solution)/shard_map/all_to_all | solution.py:264
  43.7 4.8 %copy-start.5 = (bf16[80,32,80]{2,0,1:T(8,128)(2,1)}, bf16[80,32,80]{2,0,1:T(8,128)(2,1)S(1)}, u32[]{:S(2)}) copy-start(bf16[80,32,80]{2,0,1:T(8,128)(2,1)S(1)} %copy.13) | copy-start | bytes 1228804
  48.8 61.1 %copy-start = (bf16[640,1536]{1,0:T(8,128)(2,1)S(1)}, bf16[640,1536]{1,0:T(8,128)(2,1)}, u32[]{:S(2)}) copy-start(bf16[640,1536]{1,0:T(8,128)(2,1)} %codes_hbm.3) | copy-start | bytes 5898244
  48.8 61.1 %copy-start.1 = (bf16[3,512,512]{2,1,0:T(8,128)(2,1)S(1)}, bf16[3,512,512]{2,1,0:T(8,128)(2,1)}, u32[]{:S(2)}) copy-start(bf16[3,512,512]{2,1,0:T(8,128)(2,1)} %diag_hbm.3) | copy-start | bytes 4718596
  48.8 61.0 %copy-start.4 = (f32[640]{0:T(1024)S(1)}, f32[640]{0:T(1024)}, u32[]{:S(2)}) copy-start(f32[640]{0:T(1024)} %param.11) | copy-start | bytes 7684
  109.8 1.1 copy-start.3

commit v4 on v3

--- a/solution.py
+++ b/solution.py
@@ -9,6 +9,7 @@
 
 LANES = 128
 HALF = 64
+SPLIT = 80
 F32 = jnp.float32
 BF16 = jnp.bfloat16
 MIB = 1024 * 1024
@@ -86,11 +87,11 @@
         columns = slice(block * block_len, (block + 1) * block_len)
         forward_ref[:, columns] = dot(rhs[:, columns], diag[block]).astype(BF16)
     copies[-1].wait()
+    coupled_sums = dot(codes[...], forward_ref[...], 1, 1)
     for group in range(0, rows, LANES):
         span = slice(group, min(group + LANES, rows))
         count = span.stop - span.start
-        value = dot(codes[span, :], forward_ref[...], 1, 1)
-        value = value * factors[:count, group // LANES : group // LANES + 1]
+        value = coupled_sums[span, :] * factors[:count, group // LANES : group // LANES + 1]
         coupled[span, :LANES] = value[:, :LANES]
         tail = value[:, LANES:]
         coupled[span, LANES : LANES + HALF] = tail
@@ -108,7 +109,7 @@
     chunks_ref[...] = packed[...].astype(BF16)
 
 
-def sum_kernel(per_share, chunks_ref, hot_ref, sums_ref, wide, table, total):
+def sum_kernel(per_share, chunks_ref, hot_ref, sums_ref, wide, table, total, early, late):
     peers, chunk_rows = chunks_ref.shape[0], chunks_ref.shape[1]
     members, own_pad = sums_ref.shape[0], sums_ref.shape[1]
     half = per_share // 2
@@ -135,26 +136,109 @@
     result = dot(values, hot_ref[...])
     total[:LANES, :] = result[:, :LANES]
     total[LANES:, :] = result[:HALF, LANES : 2 * LANES] + result[HALF:, 2 * LANES :]
-    own = total.shape[0] // members
-    if own < own_pad:
-        sums_ref[...] = jnp.zeros_like(sums_ref)
+    value = total[...]
+    early[...] = pltpu.roll(value, SPLIT, 1)
+    late[...] = pltpu.roll(value, SPLIT // 2, 1)
+    quad = own_pad // 2
+    lane = lax.broadcasted_iota(jnp.int32, (quad, LANES), 1)
     for member in range(members):
-        sums_ref[member, :own, :] = total[member * own : (member + 1) * own, :].astype(BF16)
-
-
-def spread_kernel(own, solved_ref, solution_ref, picker_ref, wide, total):
-    members = solved_ref.shape[0]
-    wide[...] = solved_ref[...].astype(F32)
+        first = member * 3 * quad
+        for part, moved in enumerate((early, late)):
+            extra = jnp.where(lane < SPLIT * 3 // 2, moved[first + 2 * quad : first + 3 * quad, :], 0.0)
+            begin = first + part * quad
+            sums_ref[member, part * quad : (part + 1) * quad, :] = jnp.where(
+                lane < SPLIT, total[begin : begin + quad, :], extra
+            )
+
+
+def weights_kernel(root_ref, weights_ref):
+    share_len, sep_len = root_ref.shape
+    lane = lax.broadcasted_iota(jnp.int32, (share_len, LANES), 1)
+    beside = jnp.logical_and(lane >= SPLIT, lane < SPLIT * 3 // 2)
+    weights_ref[3 * share_len :, :] = jnp.zeros_like(weights_ref[3 * share_len :, :])
+    for peer in range(sep_len // share_len):
+        base = peer * share_len // LANES * LANES
+        shift = peer * share_len - base
+        width = LANES if shift + share_len <= LANES else 2 * LANES
+        block = root_ref[:, base : base + width].astype(F32)
+        if shift:
+            block = pltpu.roll(block, width - shift, 1)
+        block = block[:, :LANES]
+        columns = slice(peer * LANES, (peer + 1) * LANES)
+        plain = jnp.where(lane < SPLIT, block, 0.0)
+        first = jnp.where(beside, pltpu.roll(block, SPLIT, 1), 0.0)
+        second = jnp.where(beside, pltpu.roll(block, SPLIT // 2, 1), 0.0)
+        weights_ref[:share_len, columns] = plain.astype(BF16)
+        weights_ref[share_len : 2 * share_len, columns] = first.astype(BF16)
+        weights_ref[2 * share_len : 3 * share_len, columns] = second.astype(BF16)
+
+
+def root_forward_kernel(sums_ref, right_ref, weights_ref, parts_ref):
+    gathered = jnp.sum(sums_ref[...], axis=0)
+    residue = (right_ref[...] - gathered).astype(BF16).astype(F32)
+    row = lax.broadcasted_iota(jnp.int32, residue.shape, 0)
+    lane = lax.broadcasted_iota(jnp.int32, residue.shape, 1)
+    top = row < 4
+    near = pltpu.roll(residue, LANES - SPLIT, 1)
+    far = pltpu.roll(residue, LANES - SPLIT // 2, 1)
+    upper = jnp.where(lane < SPLIT // 2, near, pltpu.roll(far, 4, 0))
+    lower = jnp.where(lane < SPLIT // 2, pltpu.roll(near, 4, 0), far)
+    whole = lane < SPLIT
+    upper = pltpu.roll(jnp.where(jnp.logical_and(whole, top), upper, 0.0), SPLIT, 1)
+    lower = jnp.where(jnp.logical_and(whole, jnp.logical_not(top)), lower, 0.0)
+    lower = pltpu.roll(lower, 2 * SPLIT - LANES, 1)
+    left = jnp.where(whole, residue, upper)
+    right = jnp.where(lane < 2 * SPLIT - LANES, upper, lower)
+    operand = jnp.concatenate([left, right], axis=1).astype(BF16)
+    result = dot(operand, weights_ref[...]).astype(BF16)
+    for peer in range(parts_ref.shape[0]):
+        parts_ref[peer] = result[:, peer * LANES : (peer + 1) * LANES]
+
+
+def root_backward_kernel(forward_ref, weights_ref, solved_ref):
+    peers = forward_ref.shape[0]
+    operand = jnp.concatenate([forward_ref[peer] for peer in range(peers)], axis=1)
+    result = dot(operand, weights_ref[...], 1, 1)
+    left, right = result[:, :LANES], result[:, LANES:]
+    row = lax.broadcasted_iota(jnp.int32, left.shape, 0)
+    lane = lax.broadcasted_iota(jnp.int32, left.shape, 1)
+    gap = LANES - SPLIT
+    first = jnp.where(lane < gap, pltpu.roll(left, gap, 1), pltpu.roll(right, gap, 1))
+    second = pltpu.roll(right, LANES - (2 * SPLIT - LANES), 1)
+    third = first + pltpu.roll(second, 4, 0)
+    beside = jnp.where(
+        row < 4, pltpu.roll(third, SPLIT, 1), pltpu.roll(pltpu.roll(third, SPLIT // 2, 1), 4, 0)
+    )
+    packed = jnp.where(lane < SPLIT, left, jnp.where(lane < SPLIT * 3 // 2, beside, 0.0))
+    solved_ref[...] = jnp.broadcast_to(packed.astype(BF16)[None], solved_ref.shape)
+
+
+def spread_kernel(solved_ref, hot_ref, solution_ref, picked_ref, wide, total, picker):
+    members, rows = solved_ref.shape[0], solved_ref.shape[1]
+    quad = rows // 2
+    plain = solved_ref[...].astype(F32).reshape(members * rows, LANES)
+    wide[0] = plain
+    wide[1] = pltpu.roll(plain, LANES - SPLIT, 1)
+    wide[2] = pltpu.roll(plain, LANES - SPLIT // 2, 1)
+    lane = lax.broadcasted_iota(jnp.int32, (quad, LANES), 1)
     for member in range(members):
-        total[member * own : (member + 1) * own, :] = wide[member, :own, :]
-    value = total[...]
+        first, place = member * rows, member * 3 * quad
+        total[place : place + rows, :] = wide[0, first : first + rows, :]
+        total[place + rows : place + rows + quad, :] = jnp.where(
+            lane < SPLIT // 2,
+            wide[1, first : first + quad, :],
+            wide[2, first + quad : first + rows, :],
+        )
+    value = jnp.where(lax.broadcasted_iota(jnp.int32, total.shape, 1) < SPLIT, total[...], 0.0)
     tail = value[LANES:, :].astype(BF16)
     nothing = jnp.zeros((HALF, LANES), BF16)
-    picker_ref[:, :LANES] = value[:LANES, :].astype(BF16)
-    picker_ref[:HALF, LANES : 2 * LANES] = tail
-    picker_ref[HALF:, LANES : 2 * LANES] = nothing
-    picker_ref[:HALF, 2 * LANES :] = nothing
-    picker_ref[HALF:, 2 * LANES :] = tail
+    picker[:, :LANES] = value[:LANES, :].astype(BF16)
+    picker[:HALF, LANES : 2 * LANES] = tail
+    picker[HALF:, LANES : 2 * LANES] = nothing
+    picker[:HALF, 2 * LANES :] = nothing
+    picker[HALF:, 2 * LANES :] = tail
+    picked = dot(hot_ref[...], picker[...], 1, 1).astype(BF16)
+    picked_ref[...] = picked.reshape(picked_ref.shape)
     padded = jnp.concatenate([value, jnp.zeros((HALF, LANES), F32)], axis=0)
     flipped = padded.T
     solution_ref[...] = flipped[: solution_ref.shape[0], : solution_ref.shape[1]]
@@ -217,7 +301,8 @@
     per_share = coupled_rows // tile_count
     chunk_rows = round_up(per_share + per_share // 2 + 1, 16)
     own_rhs = rhs_count // grid_count
-    own_pad = round_up(own_rhs, 16)
+    own_pad = own_rhs * 2 // 3
+    assert own_rhs == 12 and share_len == SPLIT and rhs_count == LANES + HALF
 
     groups = -(-coupled_rows // LANES)
     scales = jnp.pad(row_scales, (0, groups * LANES - coupled_rows)).reshape(groups, LANES)
@@ -248,7 +333,7 @@
         functools.partial(sum_kernel, per_share),
         out_shape=(
             jax.ShapeDtypeStruct((tile_count * chunk_rows, 3 * LANES), BF16),
-            jax.ShapeDtypeStruct((grid_count, own_pad, LANES), BF16),
+            jax.ShapeDtypeStruct((grid_count, own_pad, LANES), F32),
         ),
         in_specs=[VMEM],
         out_specs=(VMEM, VMEM),
@@ -256,47 +341,67 @@
             pltpu.VMEM((tile_count, chunk_rows, LANES), F32),
             pltpu.VMEM((LANES, LANES), F32),
             pltpu.VMEM((rhs_count, LANES), F32),
+            pltpu.VMEM((rhs_count, LANES), F32),
+            pltpu.VMEM((rhs_count, LANES), F32),
         ],
         compiler_params=params(8 * MIB),
         cost_estimate=cost(2 * tile_count * chunk_rows * 3 * LANES * LANES, 1 << 20),
         name="gather_sum",
     )(arrived)
-    own_share = lax.all_to_all(sums, "grid", 0, 0, tiled=True).astype(F32).sum(axis=0)
-    own_right = lax.dynamic_slice_in_dim(rhs_sep, lax.axis_index("grid") * own_rhs, own_rhs, 0)
-    own_right = jnp.pad(own_right, ((0, own_pad - own_rhs), (0, LANES - share_len)))
-    residue = (own_right.astype(F32) - own_share)[:, :share_len].astype(BF16)
-    spaced = root_inv.reshape(share_len, tile_count, share_len)
-    spaced = jnp.pad(spaced, ((0, 0), (0, 0), (0, LANES - share_len)))
-    spaced = spaced.reshape(share_len, tile_count * LANES)
-    root_part = jnp.dot(residue, spaced, preferred_element_type=F32).astype(BF16)
-    root_part = root_part.reshape(own_pad, tile_count, LANES).transpose(1, 0, 2)
+    weight_rows = round_up(3 * share_len, LANES)
+    weights = pl.pallas_call(
+        weights_kernel,
+        out_shape=jax.ShapeDtypeStruct((weight_rows, tile_count * LANES), BF16),
+        in_specs=[VMEM],
+        out_specs=VMEM,
+        compiler_params=params(4 * MIB),
+        cost_estimate=cost(share_len * sep_len * 16, 3 << 20),
+        name="weights",
+    )(root_inv)
+    arrived_sums = lax.all_to_all(sums, "grid", 0, 0, tiled=True)
+    right = lax.dynamic_slice_in_dim(rhs_sep, lax.axis_index("grid") * own_rhs, own_rhs, 0)
+    beside = jnp.concatenate([right[own_pad:, : SPLIT // 2], right[own_pad:, SPLIT // 2 :]], axis=0)
+    right = jnp.concatenate([right[:own_pad], beside], axis=1).astype(F32)
+    right = jnp.pad(right, ((0, 0), (0, LANES - right.shape[1])))
+    root_part = pl.pallas_call(
+        root_forward_kernel,
+        out_shape=jax.ShapeDtypeStruct((tile_count, own_pad, LANES), BF16),
+        in_specs=[VMEM, VMEM, VMEM],
+        out_specs=VMEM,
+        compiler_params=params(4 * MIB),
+        cost_estimate=cost(2 * own_pad * weight_rows * tile_count * LANES, 2 << 20),
+        name="root_forward",
+    )(arrived_sums, right, weights)
     forward_sep = lax.all_to_all(root_part, "tile", 0, 0, tiled=True).astype(F32).sum(axis=0)
-    forward_sep = jnp.broadcast_to(
-        forward_sep.astype(BF16)[None], (tile_count, own_pad, LANES)
-    )
+    forward_sep = jnp.broadcast_to(forward_sep.astype(BF16)[None], (tile_count, own_pad, LANES))
     forward_sep = lax.all_to_all(forward_sep, "tile", 0, 0, tiled=True)
-    forward_sep = forward_sep.transpose(1, 0, 2).reshape(own_pad, tile_count * LANES)
-    solved = dot(forward_sep, spaced, 1, 1)
-    solved = jnp.pad(solved.astype(BF16), ((0, 0), (0, LANES - share_len)))
-    solved = jnp.broadcast_to(solved[None], (grid_count, own_pad, LANES))
+    solved = pl.pallas_call(
+        root_backward_kernel,
+        out_shape=jax.ShapeDtypeStruct((grid_count, own_pad, LANES), BF16),
+        in_specs=[VMEM, VMEM],
+        out_specs=VMEM,
+        compiler_params=params(4 * MIB),
+        cost_estimate=cost(2 * own_pad * weight_rows * tile_count * LANES, 2 << 20),
+        name="root_backward",
+    )(forward_sep, weights)
     solved = lax.all_to_all(solved, "grid", 0, 0, tiled=True)
-    solution_sep, picker = pl.pallas_call(
-        functools.partial(spread_kernel, own_rhs),
+    solution_sep, picked = pl.pallas_call(
+        spread_kernel,
         out_shape=(
             jax.ShapeDtypeStruct((share_len, rhs_count), F32),
-            jax.ShapeDtypeStruct((LANES, 3 * LANES), BF16),
+            jax.ShapeDtypeStruct((tile_count, chunk_rows, LANES), BF16),
         ),
-        in_specs=[VMEM],
+        in_specs=[VMEM, VMEM],
         out_specs=(VMEM, VMEM),
         scratch_shapes=[
-            pltpu.VMEM((grid_count, own_pad, LANES), F32),
+            pltpu.VMEM((3, grid_count * own_pad, LANES), F32),
             pltpu.VMEM((rhs_count, LANES), F32),
+            pltpu.VMEM((LANES, 3 * LANES), BF16),
         ],
-        compiler_params=params(4 * MIB),
+        compiler_params=params(6 * MIB),
+        cost_estimate=cost(2 * tile_count * chunk_rows * 3 * LANES * LANES, 1 << 20),
         name="spread",
-    )(solved)
-    picked = dot(onehot, picker, 1, 1).astype(BF16)
-    picked = picked.reshape(tile_count, chunk_rows, LANES)
+    )(solved, onehot)
     picked = lax.all_to_all(picked, "tile", 0, 0, tiled=True)
     result = pl.pallas_call(
         functools.partial(backward_kernel, per_share),

time: 115 us -> 110 us (0.957)
  blocking collectives: 81.2 us -> 55.1 us
  starting transfers between devices: 7.2 us -> 19.8 us
  waiting for transfers between devices: 4.78 us -> 14.8 us
  Pallas kernels: 10.6 us -> 14 us
  matrix products: 3.04 us -> 0 us
  local copies, waits for them, and re-layouts: 5.05 us -> 2.97 us
    all_to_all x1 -> x0, blocking collectives: 24.9 us -> none  [on_device(): arrived = lax.all_to_all(chunks, 'tile', 0, 0, tiled=True)]
    all_to_all x1 -> x2, starting transfers between devices: 7.2 us -> 19.8 us  [the longest x1 12.6 us: on_device(): arrived = lax.all_to_all(chunks, 'tile', 0, 0, tiled=True)]
    all_to_all x1 -> x2, waiting for transfers between devices: 4.78 us -> 14.8 us  [the longest x1 11.4 us: on_device(): arrived = lax.all_to_all(chunks, 'tile', 0, 0, tiled=True)]
    pallas_call x1 -> x4, Pallas kernels: 0.74 us -> 4.59 us  [the longest x1 2.25 us: on_device(): pl.pallas_call(weights_kernel, out_shape=jax.ShapeDtypeStruct((weight_row...]
    dot_general x3 -> x0, matrix products: 3.04 us -> none  [the longest x2 2.85 us: dot(): lax.dot_general(left, right, (((left_dim,), (right_dim,)), ((), ())), pre...]
    reshape x3 -> x0, local copies, waits for them, and re-layouts: 2.07 us -> none  [the longest x2 2.04 us: on_device(): spaced = root_inv.reshape(share_len, tile_count, share_len)]
    slice x0 -> x2, local copies, waits for them, and re-layouts: none -> 1.67 us  [the longest x1 0.86 us: on_device(): right = jnp.concatenate([right[:own_pad], beside], axis=1).astype(F32)]
    all_to_all x1, blocking collectives: 15 us -> 13.7 us  [on_device(): lax.all_to_all(root_part, 'tile', 0, 0, tiled=True).astype(F32).sum(axis=0)]
  transfers between devices with their start and end apart: 1 -> 2, of which waited for: 1 -> 2; matrix products, arithmetic and copies ran while one was open for 3% -> 2% of each run, Pallas kernels for 0% -> 2%
where the time goes in v4:
time: 110 us; the launch traced here: 109 us
  blocking collectives  55.1 us (50%)
  starting transfers between devices  19.8 us (18%)
  waiting for transfers between devices  14.8 us (13%)
  Pallas kernels  14 us (13%)
  local copies, waits for them, and re-layouts  2.97 us (3%)
  between operations  1.36 us (1%)
    all_to_all x1, blocking collectives, on_device(): picked = lax.all_to_all(picked, 'tile', 0, 0, tiled=True)  16.7 us
    all_to_all x1, blocking collectives, on_device(): lax.all_to_all(root_part, 'tile', 0, 0, tiled=True).astype(F32).sum(axis=0)  13.7 us
    all_to_all x1, blocking collectives, on_device(): forward_sep = lax.all_to_all(forward_sep, 'tile', 0, 0, tiled=True)  13.3 us
    all_to_all x1, starting transfers between devices, on_device(): arrived = lax.all_to_all(chunks, 'tile', 0, 0, tiled=True)  12.6 us
    all_to_all x1, waiting for transfers between devices, on_device(): arrived = lax.all_to_all(chunks, 'tile', 0, 0, tiled=True)  11.4 us
    all_to_all x1, blocking collectives, on_device(): solved = lax.all_to_all(solved, 'grid', 0, 0, tiled=True)  11.3 us
    all_to_all x1, starting transfers between devices, on_device(): arrived_sums = lax.all_to_all(sums, 'grid', 0, 0, tiled=True)  7.2 us
    pallas_call x1, Pallas kernels, on_device(): pl.pallas_call(functools.partial(forward_kernel, per_share, share_len), o...  4.58 us
  transfers between devices with their start and end apart: 2, of which 2 were waited for; matrix products, arithmetic and copies ran while one was open for 2% of the time, Pallas kernels for 2%

profile of v4, /device:TPU:64, one launch (start us, length us, event | category | flops | bytes accessed | tf_op | source)
XLA Modules:
  0.0 109.0 jit_solution(11412876891510547803)
XLA Ops:
  1.3 4.6 %forward.1 = (bf16[192,1536]{1,0:T(8,128)(2,1)}, bf16[32,32,128]{2,1,0:T(8,128)(2,1)}) custom-call(bf16[192,1536]{1,0:T(8,128)(2,1)} %rhs_hbm.1, bf16[3,512,512]{2,1,0:T(8,128)(2,1)} %diag_hbm.3, bf16[640,1536]{1,0:T(8,128)(2,1)} %codes_hbm.3, f32[5,128]{1,0:T(8,128)} %bitcast.3, s32[5,128]{1,0:T(8,128)} %bitcast.5, s32[1]{0:T(128)S(6)} %copy.15.live_ref), custom_call_target="tpu_custom_call" | custom-call | flops 679477248 | bytes 5242880 | tf_op jit(solution)/shard_map/forward/pallas_call | solution.py:311
  5.9 12.6 %all-to-all-start = ((bf16[32,32,128]{2,1,0:T(8,128)(2,1)}), bf16[32,32,128]{2,1,0:T(8,128)(2,1)S(1)}, u32[]{:S(2)}, u32[]{:S(2)}) async-start(bf16[32,32,128]{2,1,0:T(8,128)(2,1)} %get-tuple-element.8), calls=%async_computation | async-start | bytes 524288 | tf_op jit(solution)/shard_map/all_to_all | solution.py:331
  18.5 0.9 constant_dynamic-slice_fusion.1
  19.3 11.4 %all-to-all-done.chunks_ref = bf16[32,32,128]{2,1,0:T(8,128)(2,1)S(1)} async-done(((bf16[32,32,128]{2,1,0:T(8,128)(2,1)}), bf16[32,32,128]{2,1,0:T(8,128)(2,1)S(1)}, u32[]{:S(2)}, u32[]{:S(2)}) %all-to-all-start) | async-done | bytes 262176 | tf_op jit(solution)/shard_map/all_to_all | solution.py:331
  30.7 1.5 %gather_sum.1 = (bf16[1024,384]{1,0:T(8,128)(2,1)S(1)}, f32[16,8,128]{2,1,0:T(8,128)}) custom-call(bf16[32,32,128]{2,1,0:T(8,128)(2,1)S(1)} %all-to-all-done.chunks_ref), custom_call_target="tpu_custom_call" | custom-call | flops 100663296 | bytes 1048576 | tf_op jit(solution)/shard_map/gather_sum/pallas_call | solution.py:332
  32.2 7.2 %all-to-all-start.1 = ((f32[16,8,128]{2,1,0:T(8,128)}), f32[16,8,128]{2,1,0:T(8,128)S(1)}, u32[]{:S(2)}, u32[]{:S(2)}) async-start(f32[16,8,128]{2,1,0:T(8,128)} %get-tuple-element.9), calls=%async_computation.1 | async-start | bytes 131072 | tf_op jit(solution)/shard_map/all_to_all | solution.py:361
  39.4 0.8 constant_dynamic-slice_fusion
  40.3 0.1 copy.13
  40.3 0.1 copy.14
  40.4 0.1 copy.12
  40.5 1.0 copy-done.3
  41.5 2.3 %weights.1.weights_ref = bf16[256,4096]{1,0:T(8,128)(2,1)S(1)} custom-call(bf16[80,2560]{1,0:T(8,128)(2,1)S(1)} %copy-done.3), custom_call_target="tpu_custom_call" | custom-call | flops 3276800 | bytes 3145728 | tf_op jit(solution)/shard_map/weights/pallas_call | solution.py:352
  43.8 0.1 fusion.4.right_ref
  43.9 3.4 %all-to-all-done.1.sums_ref = f32[16,8,128]{2,1,0:T(8,128)S(1)} async-done(((f32[16,8,128]{2,1,0:T(8,128)}), f32[16,8,128]{2,1,0:T(8,128)S(1)}, u32[]{:S(2)}, u32[]{:S(2)}) %all-to-all-start.1) | async-done | bytes 65568 | tf_op jit(solution)/shard_map/all_to_all | solution.py:361
  47.2 0.5 root_forward.1
  47.7 13.7 %all_to_all.30 = bf16[32,8,128]{2,1,0:T(8,128)(2,1)} all-to-all(bf16[32,8,128]{2,1,0:T(8,128)(2,1)S(1)} %root_forward.1), channel_id=1, replica_groups=mesh['grid'=16,'tile'=32] {'tile'}, dimensions={0} | all-to-all | bytes 131072 | tf_op jit(solution)/shard_map/all_to_all | solution.py:375
  61.4 0.9 reduce_sum.12
  62.3 0.0 copy-start.1
  62.4 13.3 %all_to_all.31.forward_ref = bf16[32,8,128]{2,1,0:T(8,128)(2,1)S(1)} all-to-all(bf16[32,8,128]{2,1,0:T(8,128)(2,1)S(1)} %broadcast_in_dim.2), channel_id=1, replica_groups=mesh['grid'=16,'tile'=32] {'tile'}, dimensions={0} | all-to-all | bytes 131072 | tf_op jit(solution)/shard_map/all_to_all | solution.py:377
  75.7 0.8 root_backward.1
  76.5 11.3 %all_to_all.32.solved_ref = bf16[16,8,128]{2,1,0:T(8,128)(2,1)S(1)} all-to-all(bf16[16,8,128]{2,1,0:T(8,128)(2,1)S(1)} %root_backward.1), channel_id=1, replica_groups=mesh['grid'=16,'tile'=32] {'grid'}, dimensions={0} | all-to-all | bytes 65536 | tf_op jit(solution)/shard_map/all_to_all | solution.py:387
  87.8 1.1 spread.1
  88.8 16.7 %all_to_all.33.chunks_ref = bf16[32,32,128]{2,1,0:T(8,128)(2,1)S(1)} all-to-all(bf16[32,32,128]{2,1,0:T(8,128)(2,1)S(1)} %get-tuple-element.11), channel_id=1, replica_groups=mesh['grid'=16,'tile'=32] {'tile'}, dimensions={0} | all-to-all | bytes 524288 | tf_op jit(solution)/shard_map/all_to_all | solution.py:405
  105.6 3.4 %backward.1 = bf16[192,1536]{1,0:T(8,128)(2,1)} custom-call(bf16[32,32,128]{2,1,0:T(8,128)(2,1)S(1)} %all_to_all.33.chunks_ref, f32[5,128]{1,0:T(8,128)S(1)} %bitcast.4, s32[1]{0:T(128)S(6)} %copy.15.live_ref, bf16[192,1536]{1,0:T(8,128)(2,1)S(1)} %copy-done.2, bf16[640,1536]{1,0:T(8,128)(2,1)S(1)} %copy-done, bf16[3,512,512]{2,1,0:T(8,128)(2,1)S(1)} %copy-done.1), custom_call_target="tpu_custom_call" | custom-call | flops 679477248 | bytes 5242880 | tf_op jit(solution)/shard_map/backward/pallas_call | solution.py:406
  (9 shorter events, 0.0 us)
Async XLA Ops:
  5.9 24.9 %all-to-all-start = ((bf16[32,32,128]{2,1,0:T(8,128)(2,1)}), bf16[32,32,128]{2,1,0:T(8,128)(2,1)S(1)}, u32[]{:S(2)}, u32[]{:S(2)}) async-start(bf16[32,32,128]{2,1,0:T(8,128)(2,1)} %get-tuple-element.8), calls=%async_computation | async-start | bytes 524288 | tf_op jit(solution)/shard_map/all_to_all | solution.py:331
  32.2 15.0 %all-to-all-start.1 = ((f32[16,8,128]{2,1,0:T(8,128)}), f32[16,8,128]{2,1,0:T(8,128)S(1)}, u32[]{:S(2)}, u32[]{:S(2)}) async-start(f32[16,8,128]{2,1,0:T(8,128)} %get-tuple-element.9), calls=%async_computation.1 | async-start | bytes 131072 | tf_op jit(solution)/shard_map/all_to_all | solution.py:361
  40.5 1.0 copy-start.3
  47.2 58.4 %copy-start.2 = (bf16[192,1536]{1,0:T(8,128)(2,1)S(1)}, bf16[192,1536]{1,0:T(8,128)(2,1)}, u32[]{:S(2)}) copy-start(bf16[192,1536]{1,0:T(8,128)(2,1)} %get-tuple-element.12.forward_ref) | copy-start | bytes 1769476
  61.4 44.2 %copy-start.4 = (f32[640]{0:T(1024)S(1)}, f32[640]{0:T(1024)}, u32[]{:S(2)}) copy-start(f32[640]{0:T(1024)} %param.11) | copy-start | bytes 7684
  62.3 43.3 %copy-start = (bf16[640,1536]{1,0:T(8,128)(2,1)S(1)}, bf16[640,1536]{1,0:T(8,128)(2,1)}, u32[]{:S(2)}) copy-start(bf16[640,1536]{1,0:T(8,128)(2,1)} %codes_hbm.3) | copy-start | bytes 5898244
  62.3 43.3 %copy-start.1 = (bf16[3,512,512]{2,1,0:T(8,128)(2,1)S(1)}, bf16[3,512,512]{2,1,0:T(8,128)(2,1)}, u32[]{:S(2)}) copy-start(bf16[3,512,512]{2,1,0:T(8,128)(2,1)} %diag_hbm.3) | copy-start | bytes 4718596

commit v5 on v4

--- a/solution.py
+++ b/solution.py
@@ -14,7 +14,6 @@
 BF16 = jnp.bfloat16
 MIB = 1024 * 1024
 ALL_VMEM = 67043328
-ANY = pl.BlockSpec(memory_space=pl.ANY)
 VMEM = pl.BlockSpec(memory_space=pltpu.VMEM)
 SMEM = pl.BlockSpec(memory_space=pltpu.SMEM)
 HBM = pl.BlockSpec(memory_space=pltpu.HBM)
@@ -76,12 +75,13 @@
             pltpu.make_async_copy(diag_hbm.at[block], diag.at[block], sems.at[1 + block])
         )
     copies.append(pltpu.make_async_copy(codes_hbm, codes, sems.at[1 + blocks]))
-    for copy in copies:
+    for copy in copies[:-1]:
         copy.start()
     factors = factor_columns(scales_ref, live_ref)
     offsets = offset_rows(index_ref, rows // per_share, per_share, share_len)
     packed[...] = jnp.zeros_like(packed)
     copies[0].wait()
+    copies[-1].start()
     for block in range(blocks):
         copies[1 + block].wait()
         columns = slice(block * block_len, (block + 1) * block_len)
@@ -195,6 +195,11 @@
         parts_ref[peer] = result[:, peer * LANES : (peer + 1) * LANES]
 
 
+def root_middle_kernel(parts_ref, forward_ref):
+    total = jnp.sum(parts_ref[...].astype(F32), axis=0).astype(BF16)
+    forward_ref[...] = jnp.broadcast_to(total[None], forward_ref.shape)
+
+
 def root_backward_kernel(forward_ref, weights_ref, solved_ref):
     peers = forward_ref.shape[0]
     operand = jnp.concatenate([forward_ref[peer] for peer in range(peers)], axis=1)
@@ -245,20 +250,11 @@
 
 
 def backward_kernel(
-    per_share, chunks_ref, scales_ref, live_ref, forward_ref, codes_hbm, diag_hbm,
-    result_ref,
-    codes, diag, wide, picked, sems,
+    per_share, chunks_ref, scales_ref, live_ref, forward_ref, codes, diag, result_ref, wide, picked
 ):
     blocks, block_len = diag.shape[0], diag.shape[1]
     rows, rhs_count = codes.shape[0], forward_ref.shape[0]
     half = per_share // 2
-    copies = [pltpu.make_async_copy(codes_hbm, codes, sems.at[0])]
-    for block in range(blocks):
-        copies.append(
-            pltpu.make_async_copy(diag_hbm.at[block], diag.at[block], sems.at[1 + block])
-        )
-    for copy in copies:
-        copy.start()
     factors = factor_columns(scales_ref, live_ref)
     wide[...] = chunks_ref[...].astype(F32)
     for peer in range(rows // per_share):
@@ -274,12 +270,10 @@
         value = picked[span, :] * factors[:count, group // LANES : group // LANES + 1]
         weighted.append(value.T[:rhs_count].astype(BF16))
     weighted = jnp.concatenate(weighted, axis=1)
-    copies[0].wait()
     for block in range(blocks):
         columns = slice(block * block_len, (block + 1) * block_len)
         update = dot(weighted, codes[:, columns])
         misfit = (forward_ref[:, columns].astype(F32) - update).astype(BF16)
-        copies[1 + block].wait()
         result_ref[:, columns] = dot(misfit, diag[block], 1, 1).astype(BF16)
 
 
@@ -329,6 +323,21 @@
         name="forward",
     )(rhs_local, diag_inv, codes, scales, indices, live_rows)
     arrived = lax.all_to_all(chunks, "tile", 0, 0, tiled=True)
+    weight_rows = round_up(3 * share_len, LANES)
+    weights = pl.pallas_call(
+        weights_kernel,
+        out_shape=jax.ShapeDtypeStruct((weight_rows, tile_count * LANES), BF16),
+        in_specs=[VMEM],
+        out_specs=VMEM,
+        compiler_params=params(4 * MIB),
+        cost_estimate=cost(share_len * sep_len * 16, 3 << 20),
+        name="weights",
+    )(root_inv)
+    right = lax.dynamic_slice_in_dim(rhs_sep, lax.axis_index("grid") * own_rhs, own_rhs, 0)
+    beside = jnp.concatenate([right[own_pad:, : SPLIT // 2], right[own_pad:, SPLIT // 2 :]], axis=0)
+    right = jnp.concatenate([right[:own_pad], beside], axis=1).astype(F32)
+    right = jnp.pad(right, ((0, 0), (0, LANES - right.shape[1])))
+    arrived, weights, right = lax.optimization_barrier((arrived, weights, right))
     onehot, sums = pl.pallas_call(
         functools.partial(sum_kernel, per_share),
         out_shape=(
@@ -348,21 +357,7 @@
         cost_estimate=cost(2 * tile_count * chunk_rows * 3 * LANES * LANES, 1 << 20),
         name="gather_sum",
     )(arrived)
-    weight_rows = round_up(3 * share_len, LANES)
-    weights = pl.pallas_call(
-        weights_kernel,
-        out_shape=jax.ShapeDtypeStruct((weight_rows, tile_count * LANES), BF16),
-        in_specs=[VMEM],
-        out_specs=VMEM,
-        compiler_params=params(4 * MIB),
-        cost_estimate=cost(share_len * sep_len * 16, 3 << 20),
-        name="weights",
-    )(root_inv)
     arrived_sums = lax.all_to_all(sums, "grid", 0, 0, tiled=True)
-    right = lax.dynamic_slice_in_dim(rhs_sep, lax.axis_index("grid") * own_rhs, own_rhs, 0)
-    beside = jnp.concatenate([right[own_pad:, : SPLIT // 2], right[own_pad:, SPLIT // 2 :]], axis=0)
-    right = jnp.concatenate([right[:own_pad], beside], axis=1).astype(F32)
-    right = jnp.pad(right, ((0, 0), (0, LANES - right.shape[1])))
     root_part = pl.pallas_call(
         root_forward_kernel,
         out_shape=jax.ShapeDtypeStruct((tile_count, own_pad, LANES), BF16),
@@ -372,8 +367,14 @@
         cost_estimate=cost(2 * own_pad * weight_rows * tile_count * LANES, 2 << 20),
         name="root_forward",
     )(arrived_sums, right, weights)
-    forward_sep = lax.all_to_all(root_part, "tile", 0, 0, tiled=True).astype(F32).sum(axis=0)
-    forward_sep = jnp.broadcast_to(forward_sep.astype(BF16)[None], (tile_count, own_pad, LANES))
+    forward_sep = pl.pallas_call(
+        root_middle_kernel,
+        out_shape=jax.ShapeDtypeStruct((tile_count, own_pad, LANES), BF16),
+        in_specs=[VMEM],
+        out_specs=VMEM,
+        compiler_params=params(2 * MIB),
+        name="root_middle",
+    )(lax.all_to_all(root_part, "tile", 0, 0, tiled=True))
     forward_sep = lax.all_to_all(forward_sep, "tile", 0, 0, tiled=True)
     solved = pl.pallas_call(
         root_backward_kernel,
@@ -406,14 +407,11 @@
     result = pl.pallas_call(
         functools.partial(backward_kernel, per_share),
         out_shape=jax.ShapeDtypeStruct((rhs_count, local_len), BF16),
-        in_specs=[VMEM, VMEM, SMEM, VMEM, ANY, ANY],
+        in_specs=[VMEM, VMEM, SMEM, VMEM, VMEM, VMEM],
         out_specs=VMEM,
         scratch_shapes=[
-            pltpu.VMEM(codes.shape, BF16),
-            pltpu.VMEM(diag_inv.shape, BF16),
             pltpu.VMEM((tile_count, chunk_rows, LANES), F32),
             pltpu.VMEM((coupled_rows, 2 * LANES), F32),
-            pltpu.SemaphoreType.DMA((1 + per_dev,)),
         ],
         compiler_params=params(16 * MIB),
         cost_estimate=cost(2 * rhs_count * local_len * (block_len + coupled_rows), 5 << 20),

time: 110 us -> 106 us (0.964)
  blocking collectives: 55.1 us -> 68.7 us
  waiting for transfers between devices: 14.8 us -> 6.98 us
  starting transfers between devices: 19.8 us -> 12.6 us
    all_to_all x1 -> x2, blocking collectives: 13.7 us -> 28.4 us  [the longest x1 14.8 us: on_device(): arrived_sums = lax.all_to_all(sums, 'grid', 0, 0, tiled=True)]
    all_to_all x1 -> x0, starting transfers between devices: 7.2 us -> none  [on_device(): arrived_sums = lax.all_to_all(sums, 'grid', 0, 0, tiled=True)]
    all_to_all x1, waiting for transfers between devices: 11.4 us -> 6.98 us  [on_device(): arrived = lax.all_to_all(chunks, 'tile', 0, 0, tiled=True)]
    all_to_all x1 -> x0, waiting for transfers between devices: 3.36 us -> none  [on_device(): arrived_sums = lax.all_to_all(sums, 'grid', 0, 0, tiled=True)]
  transfers between devices with their start and end apart: 2 -> 1, of which waited for: 2 -> 1; matrix products, arithmetic and copies ran while one was open for 2% -> 2% of each run, Pallas kernels for 2% -> 2%
where the time goes in v5:
time: 106 us
  blocking collectives  68.7 us (65%)
  Pallas kernels  13.1 us (12%)
  starting transfers between devices  12.6 us (12%)
  waiting for transfers between devices  6.98 us (7%)
  local copies, waits for them, and re-layouts  2.95 us (3%)
  between operations  1.34 us (1%)
    all_to_all x1, blocking collectives, on_device(): picked = lax.all_to_all(picked, 'tile', 0, 0, tiled=True)  16.7 us
    all_to_all x1, blocking collectives, on_device(): arrived_sums = lax.all_to_all(sums, 'grid', 0, 0, tiled=True)  14.8 us
    all_to_all x1, blocking collectives, on_device(): lax.all_to_all(root_part, 'tile', 0, 0, tiled=True)  13.6 us
    all_to_all x1, blocking collectives, on_device(): forward_sep = lax.all_to_all(forward_sep, 'tile', 0, 0, tiled=True)  13.3 us
    all_to_all x1, starting transfers between devices, on_device(): arrived = lax.all_to_all(chunks, 'tile', 0, 0, tiled=True)  12.6 us
    all_to_all x1, blocking collectives, on_device(): solved = lax.all_to_all(solved, 'grid', 0, 0, tiled=True)  10.3 us
    all_to_all x1, waiting for transfers between devices, on_device(): arrived = lax.all_to_all(chunks, 'tile', 0, 0, tiled=True)  6.98 us
    pallas_call x1, Pallas kernels, on_device(): pl.pallas_call(functools.partial(forward_kernel, per_share, share_len), o...  5.09 us
  transfers between devices with their start and end apart: 1, of which 1 were waited for; matrix products, arithmetic and copies ran while one was open for 2% of the time, Pallas kernels for 2%

profile of v5, /device:TPU:64, one launch (start us, length us, event | category | flops | bytes accessed | tf_op | source)
XLA Modules:
  0.0 105.7 jit_solution(6775821140048426812)
XLA Ops:
  1.3 5.1 %forward.1 = (bf16[192,1536]{1,0:T(8,128)(2,1)}, bf16[32,32,128]{2,1,0:T(8,128)(2,1)}) custom-call(bf16[192,1536]{1,0:T(8,128)(2,1)} %rhs_hbm.1, bf16[3,512,512]{2,1,0:T(8,128)(2,1)} %diag.1, bf16[640,1536]{1,0:T(8,128)(2,1)} %codes.1, f32[5,128]{1,0:T(8,128)} %bitcast.3, s32[5,128]{1,0:T(8,128)} %bitcast.5, s32[1]{0:T(128)S(6)} %copy.15.live_ref), custom_call_target="tpu_custom_call" | custom-call | flops 679477248 | bytes 5242880 | tf_op jit(solution)/shard_map/forward/pallas_call | solution.py:305
  6.4 12.6 %all-to-all-start = ((bf16[32,32,128]{2,1,0:T(8,128)(2,1)}), bf16[32,32,128]{2,1,0:T(8,128)(2,1)S(1)}, u32[]{:S(2)}, u32[]{:S(2)}) async-start(bf16[32,32,128]{2,1,0:T(8,128)(2,1)} %get-tuple-element.11), calls=%async_computation | async-start | bytes 524288 | tf_op jit(solution)/shard_map/all_to_all | solution.py:325
  19.0 0.8 constant_dynamic-slice_fusion
  19.8 0.1 copy.13
  19.9 0.1 copy.14
  20.0 0.9 constant_dynamic-slice_fusion.1
  20.8 0.1 copy.12
  20.9 1.0 copy-done.3
  21.9 2.3 %weights.1.weights_ref = bf16[256,4096]{1,0:T(8,128)(2,1)S(1)} custom-call(bf16[80,2560]{1,0:T(8,128)(2,1)S(1)} %copy-done.3), custom_call_target="tpu_custom_call" | custom-call | flops 3276800 | bytes 3145728 | tf_op jit(solution)/shard_map/weights/pallas_call | solution.py:327
  24.2 0.1 fusion.4.right_ref
  24.3 7.0 %all-to-all-done.chunks_ref = bf16[32,32,128]{2,1,0:T(8,128)(2,1)S(1)} async-done(((bf16[32,32,128]{2,1,0:T(8,128)(2,1)}), bf16[32,32,128]{2,1,0:T(8,128)(2,1)S(1)}, u32[]{:S(2)}, u32[]{:S(2)}) %all-to-all-start) | async-done | bytes 262176 | tf_op jit(solution)/shard_map/all_to_all | solution.py:325
  31.3 0.9 gather_sum.1
  32.1 14.8 %all_to_all.30.sums_ref = f32[16,8,128]{2,1,0:T(8,128)S(1)} all-to-all(f32[16,8,128]{2,1,0:T(8,128)S(1)} %get-tuple-element.13), channel_id=1, replica_groups=mesh['grid'=16,'tile'=32] {'grid'}, dimensions={0} | all-to-all | bytes 131072 | tf_op jit(solution)/shard_map/all_to_all | solution.py:360
  46.9 0.5 root_forward.1
  47.4 13.6 %all_to_all.31.parts_ref = bf16[32,8,128]{2,1,0:T(8,128)(2,1)S(1)} all-to-all(bf16[32,8,128]{2,1,0:T(8,128)(2,1)S(1)} %root_forward.1), channel_id=1, replica_groups=mesh['grid'=16,'tile'=32] {'tile'}, dimensions={0} | all-to-all | bytes 131072 | tf_op jit(solution)/shard_map/all_to_all | solution.py:377
  61.0 13.3 %all_to_all.32.forward_ref = bf16[32,8,128]{2,1,0:T(8,128)(2,1)S(1)} all-to-all(bf16[32,8,128]{2,1,0:T(8,128)(2,1)S(1)} %root_middle.1), channel_id=1, replica_groups=mesh['grid'=16,'tile'=32] {'tile'}, dimensions={0} | all-to-all | bytes 131072 | tf_op jit(solution)/shard_map/all_to_all | solution.py:378
  74.4 0.8 root_backward.1
  75.1 10.3 %all_to_all.33.solved_ref = bf16[16,8,128]{2,1,0:T(8,128)(2,1)S(1)} all-to-all(bf16[16,8,128]{2,1,0:T(8,128)(2,1)S(1)} %root_backward.1), channel_id=1, replica_groups=mesh['grid'=16,'tile'=32] {'grid'}, dimensions={0} | all-to-all | bytes 65536 | tf_op jit(solution)/shard_map/all_to_all | solution.py:388
  85.4 1.1 spread.1
  86.5 16.7 %all_to_all.34.chunks_ref = bf16[32,32,128]{2,1,0:T(8,128)(2,1)S(1)} all-to-all(bf16[32,32,128]{2,1,0:T(8,128)(2,1)S(1)} %get-tuple-element.17), channel_id=1, replica_groups=mesh['grid'=16,'tile'=32] {'tile'}, dimensions={0} | all-to-all | bytes 524288 | tf_op jit(solution)/shard_map/all_to_all | solution.py:406
  103.2 0.0 copy-done.2
  103.2 0.0 copy-done.1
  103.2 0.0 copy-done.4
  103.2 2.5 %backward.1 = bf16[192,1536]{1,0:T(8,128)(2,1)} custom-call(bf16[32,32,128]{2,1,0:T(8,128)(2,1)S(1)} %all_to_all.34.chunks_ref, f32[5,128]{1,0:T(8,128)S(1)} %bitcast.4, s32[1]{0:T(128)S(6)} %copy.15.live_ref, bf16[192,1536]{1,0:T(8,128)(2,1)S(1)} %copy-done.2, bf16[640,1536]{1,0:T(8,128)(2,1)S(1)} %copy-done, bf16[3,512,512]{2,1,0:T(8,128)(2,1)S(1)} %copy-done.1), custom_call_target="tpu_custom_call" | custom-call | flops 679477248 | bytes 5242880 | tf_op jit(solution)/shard_map/backward/pallas_call | solution.py:407
  (7 shorter events, 0.1 us)
Async XLA Ops:
  6.4 24.9 %all-to-all-start = ((bf16[32,32,128]{2,1,0:T(8,128)(2,1)}), bf16[32,32,128]{2,1,0:T(8,128)(2,1)S(1)}, u32[]{:S(2)}, u32[]{:S(2)}) async-start(bf16[32,32,128]{2,1,0:T(8,128)(2,1)} %get-tuple-element.11), calls=%async_computation | async-start | bytes 524288 | tf_op jit(solution)/shard_map/all_to_all | solution.py:325
  20.9 1.0 copy-start.3
  46.9 56.3 %copy-start.2 = (bf16[192,1536]{1,0:T(8,128)(2,1)S(1)}, bf16[192,1536]{1,0:T(8,128)(2,1)}, u32[]{:S(2)}) copy-start(bf16[192,1536]{1,0:T(8,128)(2,1)} %get-tuple-element.18.forward_ref) | copy-start | bytes 1769476
  61.0 42.2 %copy-start = (bf16[640,1536]{1,0:T(8,128)(2,1)S(1)}, bf16[640,1536]{1,0:T(8,128)(2,1)}, u32[]{:S(2)}) copy-start(bf16[640,1536]{1,0:T(8,128)(2,1)} %codes.1) | copy-start | bytes 5898244
  61.0 42.2 %copy-start.1 = (bf16[3,512,512]{2,1,0:T(8,128)(2,1)S(1)}, bf16[3,512,512]{2,1,0:T(8,128)(2,1)}, u32[]{:S(2)}) copy-start(bf16[3,512,512]{2,1,0:T(8,128)(2,1)} %diag.1) | copy-start | bytes 4718596
  61.0 42.2 %copy-start.4 = (f32[640]{0:T(1024)S(1)}, f32[640]{0:T(1024)}, u32[]{:S(2)}) copy-start(f32[640]{0:T(1024)} %param.11) | copy-start | bytes 7684

commit v6 on v5

--- a/solution.py
+++ b/solution.py
@@ -63,8 +63,8 @@
 
 def forward_kernel(
     per_share, share_len, rhs_hbm, diag_hbm, codes_hbm, scales_ref, index_ref, live_ref,
-    forward_ref, chunks_ref,
-    rhs, diag, codes, coupled, packed, sems,
+    forward_hbm, chunks_hbm,
+    rhs, diag, codes, coupled, packed, forward_ref, chunks, sems,
 ):
     blocks, block_len = diag.shape[0], diag.shape[1]
     rows, rhs_count = codes.shape[0], rhs.shape[0]
@@ -75,18 +75,19 @@
             pltpu.make_async_copy(diag_hbm.at[block], diag.at[block], sems.at[1 + block])
         )
     copies.append(pltpu.make_async_copy(codes_hbm, codes, sems.at[1 + blocks]))
-    for copy in copies[:-1]:
+    for copy in copies:
         copy.start()
     factors = factor_columns(scales_ref, live_ref)
     offsets = offset_rows(index_ref, rows // per_share, per_share, share_len)
     packed[...] = jnp.zeros_like(packed)
     copies[0].wait()
-    copies[-1].start()
     for block in range(blocks):
         copies[1 + block].wait()
         columns = slice(block * block_len, (block + 1) * block_len)
         forward_ref[:, columns] = dot(rhs[:, columns], diag[block]).astype(BF16)
     copies[-1].wait()
+    outgoing = [pltpu.make_async_copy(forward_ref, forward_hbm, sems.at[2 + blocks])]
+    outgoing[0].start()
     coupled_sums = dot(codes[...], forward_ref[...], 1, 1)
     for group in range(0, rows, LANES):
         span = slice(group, min(group + LANES, rows))
@@ -97,16 +98,26 @@
         coupled[span, LANES : LANES + HALF] = tail
         coupled[span, LANES + HALF :] = tail
     low_lane = lax.broadcasted_iota(jnp.int32, (half, LANES), 1) < HALF
-    for peer in range(rows // per_share):
-        first = peer * per_share
-        packed[peer, :per_share, :] = coupled[first : first + per_share, :LANES]
-        packed[peer, per_share : per_share + half, :] = jnp.where(
-            low_lane,
-            coupled[first : first + half, LANES:],
-            coupled[first + half : first + per_share, LANES:],
+    peers = rows // per_share
+    for part in range(2):
+        span = slice(part * peers // 2, (part + 1) * peers // 2)
+        for peer in range(span.start, span.stop):
+            first = peer * per_share
+            packed[peer, :per_share, :] = coupled[first : first + per_share, :LANES]
+            packed[peer, per_share : per_share + half, :] = jnp.where(
+                low_lane,
+                coupled[first : first + half, LANES:],
+                coupled[first + half : first + per_share, LANES:],
+            )
+            packed[peer, per_share + half : per_share + half + 1, :] = offsets[peer : peer + 1, :]
+        chunks[span] = packed[span].astype(BF16)
+        copy = pltpu.make_async_copy(
+            chunks.at[span], chunks_hbm.at[span], sems.at[3 + blocks + part]
         )
-        packed[peer, per_share + half : per_share + half + 1, :] = offsets[peer : peer + 1, :]
-    chunks_ref[...] = packed[...].astype(BF16)
+        copy.start()
+        outgoing.append(copy)
+    for copy in outgoing:
+        copy.wait()
 
 
 def sum_kernel(per_share, chunks_ref, hot_ref, sums_ref, wide, table, total, early, late):
@@ -250,7 +261,8 @@
 
 
 def backward_kernel(
-    per_share, chunks_ref, scales_ref, live_ref, forward_ref, codes, diag, result_ref, wide, picked
+    per_share, chunks_ref, scales_ref, live_ref, forward_ref, codes, diag, result_hbm,
+    wide, picked, result, sems,
 ):
     blocks, block_len = diag.shape[0], diag.shape[1]
     rows, rhs_count = codes.shape[0], forward_ref.shape[0]
@@ -270,11 +282,17 @@
         value = picked[span, :] * factors[:count, group // LANES : group // LANES + 1]
         weighted.append(value.T[:rhs_count].astype(BF16))
     weighted = jnp.concatenate(weighted, axis=1)
+    copies = []
     for block in range(blocks):
         columns = slice(block * block_len, (block + 1) * block_len)
         update = dot(weighted, codes[:, columns])
         misfit = (forward_ref[:, columns].astype(F32) - update).astype(BF16)
-        result_ref[:, columns] = dot(misfit, diag[block], 1, 1).astype(BF16)
+        result[block] = dot(misfit, diag[block], 1, 1).astype(BF16)
+        copy = pltpu.make_async_copy(result.at[block], result_hbm.at[:, columns], sems.at[block])
+        copy.start()
+        copies.append(copy)
+    for copy in copies:
+        copy.wait()
 
 
 def params(limit):
@@ -309,14 +327,16 @@
             jax.ShapeDtypeStruct((tile_count, chunk_rows, LANES), BF16),
         ),
         in_specs=[HBM, HBM, HBM, VMEM, VMEM, SMEM],
-        out_specs=(VMEM, VMEM),
+        out_specs=(HBM, HBM),
         scratch_shapes=[
             pltpu.VMEM((rhs_count, local_len), BF16),
             pltpu.VMEM(diag_inv.shape, BF16),
             pltpu.VMEM(codes.shape, BF16),
             pltpu.VMEM((coupled_rows, 2 * LANES), F32),
             pltpu.VMEM((tile_count, chunk_rows, LANES), F32),
-            pltpu.SemaphoreType.DMA((2 + per_dev,)),
+            pltpu.VMEM((rhs_count, local_len), BF16),
+            pltpu.VMEM((tile_count, chunk_rows, LANES), BF16),
+            pltpu.SemaphoreType.DMA((5 + per_dev,)),
         ],
         compiler_params=params(ALL_VMEM),
         cost_estimate=cost(2 * rhs_count * local_len * (block_len + coupled_rows), 5 << 20),
@@ -408,10 +428,12 @@
         functools.partial(backward_kernel, per_share),
         out_shape=jax.ShapeDtypeStruct((rhs_count, local_len), BF16),
         in_specs=[VMEM, VMEM, SMEM, VMEM, VMEM, VMEM],
-        out_specs=VMEM,
+        out_specs=HBM,
         scratch_shapes=[
             pltpu.VMEM((tile_count, chunk_rows, LANES), F32),
             pltpu.VMEM((coupled_rows, 2 * LANES), F32),
+            pltpu.VMEM((per_dev, rhs_count, block_len), BF16),
+            pltpu.SemaphoreType.DMA((per_dev,)),
         ],
         compiler_params=params(16 * MIB),
         cost_estimate=cost(2 * rhs_count * local_len * (block_len + coupled_rows), 5 << 20),

time: 106 us -> 106 us (level)
  no operation moved by 1% of the time
where the time goes in v6:
time: 106 us; the launch traced here: 105 us
  blocking collectives  68.7 us (65%)
  starting transfers between devices  12.6 us (12%)
  Pallas kernels  12.5 us (12%)
  waiting for transfers between devices  6.98 us (7%)
  local copies, waits for them, and re-layouts  2.95 us (3%)
  between operations  1.34 us (1%)
    all_to_all x1, blocking collectives, on_device(): picked = lax.all_to_all(picked, 'tile', 0, 0, tiled=True)  16.7 us
    all_to_all x1, blocking collectives, on_device(): arrived_sums = lax.all_to_all(sums, 'grid', 0, 0, tiled=True)  14.8 us
    all_to_all x1, blocking collectives, on_device(): lax.all_to_all(root_part, 'tile', 0, 0, tiled=True)  13.6 us
    all_to_all x1, blocking collectives, on_device(): forward_sep = lax.all_to_all(forward_sep, 'tile', 0, 0, tiled=True)  13.3 us
    all_to_all x1, starting transfers between devices, on_device(): arrived = lax.all_to_all(chunks, 'tile', 0, 0, tiled=True)  12.6 us
    all_to_all x1, blocking collectives, on_device(): solved = lax.all_to_all(solved, 'grid', 0, 0, tiled=True)  10.3 us
    all_to_all x1, waiting for transfers between devices, on_device(): arrived = lax.all_to_all(chunks, 'tile', 0, 0, tiled=True)  6.98 us
    pallas_call x1, Pallas kernels, on_device(): pl.pallas_call(functools.partial(forward_kernel, per_share, share_len), o...  4.56 us
  transfers between devices with their start and end apart: 1, of which 1 were waited for; matrix products, arithmetic and copies ran while one was open for 2% of the time, Pallas kernels for 2%

profile of v6, /device:TPU:64, one launch (start us, length us, event | category | flops | bytes accessed | tf_op | source)
XLA Modules:
  0.0 105.1 jit_solution(17255900068858596429)
XLA Ops:
  1.3 4.6 %forward.1 = (bf16[192,1536]{1,0:T(8,128)(2,1)}, bf16[32,32,128]{2,1,0:T(8,128)(2,1)}) custom-call(bf16[192,1536]{1,0:T(8,128)(2,1)} %rhs_hbm.1, bf16[3,512,512]{2,1,0:T(8,128)(2,1)} %diag.1, bf16[640,1536]{1,0:T(8,128)(2,1)} %codes.1, f32[5,128]{1,0:T(8,128)} %bitcast.3, s32[5,128]{1,0:T(8,128)} %bitcast.5, s32[1]{0:T(128)S(6)} %copy.15.live_ref), custom_call_target="tpu_custom_call" | custom-call | flops 679477248 | bytes 5242880 | tf_op jit(solution)/shard_map/forward/pallas_call | solution.py:323
  5.8 12.6 %all-to-all-start = ((bf16[32,32,128]{2,1,0:T(8,128)(2,1)}), bf16[32,32,128]{2,1,0:T(8,128)(2,1)S(1)}, u32[]{:S(2)}, u32[]{:S(2)}) async-start(bf16[32,32,128]{2,1,0:T(8,128)(2,1)} %get-tuple-element.11), calls=%async_computation | async-start | bytes 524288 | tf_op jit(solution)/shard_map/all_to_all | solution.py:345
  18.5 0.8 constant_dynamic-slice_fusion
  19.3 0.1 copy.13
  19.4 0.1 copy.14
  19.4 0.9 constant_dynamic-slice_fusion.1
  20.3 0.1 copy.12
  20.4 1.0 copy-done.3
  21.4 2.3 %weights.1.weights_ref = bf16[256,4096]{1,0:T(8,128)(2,1)S(1)} custom-call(bf16[80,2560]{1,0:T(8,128)(2,1)S(1)} %copy-done.3), custom_call_target="tpu_custom_call" | custom-call | flops 3276800 | bytes 3145728 | tf_op jit(solution)/shard_map/weights/pallas_call | solution.py:347
  23.7 0.1 fusion.4.right_ref
  23.7 7.0 %all-to-all-done.chunks_ref = bf16[32,32,128]{2,1,0:T(8,128)(2,1)S(1)} async-done(((bf16[32,32,128]{2,1,0:T(8,128)(2,1)}), bf16[32,32,128]{2,1,0:T(8,128)(2,1)S(1)}, u32[]{:S(2)}, u32[]{:S(2)}) %all-to-all-start) | async-done | bytes 262176 | tf_op jit(solution)/shard_map/all_to_all | solution.py:345
  30.7 0.9 gather_sum.1
  31.6 14.8 %all_to_all.30.sums_ref = f32[16,8,128]{2,1,0:T(8,128)S(1)} all-to-all(f32[16,8,128]{2,1,0:T(8,128)S(1)} %get-tuple-element.13), channel_id=1, replica_groups=mesh['grid'=16,'tile'=32] {'grid'}, dimensions={0} | all-to-all | bytes 131072 | tf_op jit(solution)/shard_map/all_to_all | solution.py:380
  46.4 0.5 root_forward.1
  46.9 13.6 %all_to_all.31.parts_ref = bf16[32,8,128]{2,1,0:T(8,128)(2,1)S(1)} all-to-all(bf16[32,8,128]{2,1,0:T(8,128)(2,1)S(1)} %root_forward.1), channel_id=1, replica_groups=mesh['grid'=16,'tile'=32] {'tile'}, dimensions={0} | all-to-all | bytes 131072 | tf_op jit(solution)/shard_map/all_to_all | solution.py:397
  60.5 13.3 %all_to_all.32.forward_ref = bf16[32,8,128]{2,1,0:T(8,128)(2,1)S(1)} all-to-all(bf16[32,8,128]{2,1,0:T(8,128)(2,1)S(1)} %root_middle.1), channel_id=1, replica_groups=mesh['grid'=16,'tile'=32] {'tile'}, dimensions={0} | all-to-all | bytes 131072 | tf_op jit(solution)/shard_map/all_to_all | solution.py:398
  73.8 0.8 root_backward.1
  74.6 10.3 %all_to_all.33.solved_ref = bf16[16,8,128]{2,1,0:T(8,128)(2,1)S(1)} all-to-all(bf16[16,8,128]{2,1,0:T(8,128)(2,1)S(1)} %root_backward.1), channel_id=1, replica_groups=mesh['grid'=16,'tile'=32] {'grid'}, dimensions={0} | all-to-all | bytes 65536 | tf_op jit(solution)/shard_map/all_to_all | solution.py:408
  84.9 1.1 %spread.1 = (f32[80,192]{1,0:T(8,128)}, bf16[32,32,128]{2,1,0:T(8,128)(2,1)S(1)}) custom-call(bf16[16,8,128]{2,1,0:T(8,128)(2,1)S(1)} %all_to_all.33.solved_ref, bf16[1024,384]{1,0:T(8,128)(2,1)S(1)} %get-tuple-element.16.hot_ref), custom_call_target="tpu_custom_call" | custom-call | flops 100663296 | bytes 1048576 | tf_op jit(solution)/shard_map/spread/pallas_call | solution.py:409
  85.9 16.7 %all_to_all.34.chunks_ref = bf16[32,32,128]{2,1,0:T(8,128)(2,1)S(1)} all-to-all(bf16[32,32,128]{2,1,0:T(8,128)(2,1)S(1)} %get-tuple-element.17), channel_id=1, replica_groups=mesh['grid'=16,'tile'=32] {'tile'}, dimensions={0} | all-to-all | bytes 524288 | tf_op jit(solution)/shard_map/all_to_all | solution.py:426
  102.6 0.0 copy-done.2
  102.6 0.0 copy-done
  102.6 0.0 copy-done.1
  102.7 2.4 %backward.1 = bf16[192,1536]{1,0:T(8,128)(2,1)} custom-call(bf16[32,32,128]{2,1,0:T(8,128)(2,1)S(1)} %all_to_all.34.chunks_ref, f32[5,128]{1,0:T(8,128)S(1)} %bitcast.4, s32[1]{0:T(128)S(6)} %copy.15.live_ref, bf16[192,1536]{1,0:T(8,128)(2,1)S(1)} %copy-done.2, bf16[640,1536]{1,0:T(8,128)(2,1)S(1)} %copy-done, bf16[3,512,512]{2,1,0:T(8,128)(2,1)S(1)} %copy-done.1), custom_call_target="tpu_custom_call" | custom-call | flops 679477248 | bytes 5242880 | tf_op jit(solution)/shard_map/backward/pallas_call | solution.py:427
  (7 shorter events, 0.1 us)
Async XLA Ops:
  5.8 24.9 %all-to-all-start = ((bf16[32,32,128]{2,1,0:T(8,128)(2,1)}), bf16[32,32,128]{2,1,0:T(8,128)(2,1)S(1)}, u32[]{:S(2)}, u32[]{:S(2)}) async-start(bf16[32,32,128]{2,1,0:T(8,128)(2,1)} %get-tuple-element.11), calls=%async_computation | async-start | bytes 524288 | tf_op jit(solution)/shard_map/all_to_all | solution.py:345
  20.4 1.0 copy-start.3
  46.4 56.3 %copy-start.2 = (bf16[192,1536]{1,0:T(8,128)(2,1)S(1)}, bf16[192,1536]{1,0:T(8,128)(2,1)}, u32[]{:S(2)}) copy-start(bf16[192,1536]{1,0:T(8,128)(2,1)} %get-tuple-element.18.forward_ref) | copy-start | bytes 1769476
  60.5 42.2 %copy-start = (bf16[640,1536]{1,0:T(8,128)(2,1)S(1)}, bf16[640,1536]{1,0:T(8,128)(2,1)}, u32[]{:S(2)}) copy-start(bf16[640,1536]{1,0:T(8,128)(2,1)} %codes.1) | copy-start | bytes 5898244
  60.5 42.2 %copy-start.1 = (bf16[3,512,512]{2,1,0:T(8,128)(2,1)S(1)}, bf16[3,512,512]{2,1,0:T(8,128)(2,1)}, u32[]{:S(2)}) copy-start(bf16[3,512,512]{2,1,0:T(8,128)(2,1)} %diag.1) | copy-start | bytes 4718596
  60.5 42.2 %copy-start.4 = (f32[640]{0:T(1024)S(1)}, f32[640]{0:T(1024)}, u32[]{:S(2)}) copy-start(f32[640]{0:T(1024)} %param.11) | copy-start | bytes 7684

commit v7 on v6

--- a/solution.py
+++ b/solution.py
@@ -229,7 +229,7 @@
     solved_ref[...] = jnp.broadcast_to(packed.astype(BF16)[None], solved_ref.shape)
 
 
-def spread_kernel(solved_ref, hot_ref, solution_ref, picked_ref, wide, total, picker):
+def unpack(solved_ref, wide, total):
     members, rows = solved_ref.shape[0], solved_ref.shape[1]
     quad = rows // 2
     plain = solved_ref[...].astype(F32).reshape(members * rows, LANES)
@@ -245,7 +245,11 @@
             wide[1, first : first + quad, :],
             wide[2, first + quad : first + rows, :],
         )
-    value = jnp.where(lax.broadcasted_iota(jnp.int32, total.shape, 1) < SPLIT, total[...], 0.0)
+    return jnp.where(lax.broadcasted_iota(jnp.int32, total.shape, 1) < SPLIT, total[...], 0.0)
+
+
+def spread_kernel(solved_ref, hot_ref, picked_ref, wide, total, picker):
+    value = unpack(solved_ref, wide, total)
     tail = value[LANES:, :].astype(BF16)
     nothing = jnp.zeros((HALF, LANES), BF16)
     picker[:, :LANES] = value[:LANES, :].astype(BF16)
@@ -255,16 +259,20 @@
     picker[HALF:, 2 * LANES :] = tail
     picked = dot(hot_ref[...], picker[...], 1, 1).astype(BF16)
     picked_ref[...] = picked.reshape(picked_ref.shape)
+
+
+def backward_kernel(
+    per_share, chunks_ref, scales_ref, live_ref, forward_ref, codes, diag, solved_ref,
+    result_hbm, solution_hbm,
+    wide, picked, result, solved_wide, total, solution_rows, sems,
+):
+    blocks, block_len = diag.shape[0], diag.shape[1]
+    value = unpack(solved_ref, solved_wide, total)
     padded = jnp.concatenate([value, jnp.zeros((HALF, LANES), F32)], axis=0)
     flipped = padded.T
-    solution_ref[...] = flipped[: solution_ref.shape[0], : solution_ref.shape[1]]
-
-
-def backward_kernel(
-    per_share, chunks_ref, scales_ref, live_ref, forward_ref, codes, diag, result_hbm,
-    wide, picked, result, sems,
-):
-    blocks, block_len = diag.shape[0], diag.shape[1]
+    solution_rows[...] = flipped[: solution_rows.shape[0], : solution_rows.shape[1]]
+    copies = [pltpu.make_async_copy(solution_rows, solution_hbm, sems.at[blocks])]
+    copies[0].start()
     rows, rhs_count = codes.shape[0], forward_ref.shape[0]
     half = per_share // 2
     factors = factor_columns(scales_ref, live_ref)
@@ -282,7 +290,6 @@
         value = picked[span, :] * factors[:count, group // LANES : group // LANES + 1]
         weighted.append(value.T[:rhs_count].astype(BF16))
     weighted = jnp.concatenate(weighted, axis=1)
-    copies = []
     for block in range(blocks):
         columns = slice(block * block_len, (block + 1) * block_len)
         update = dot(weighted, codes[:, columns])
@@ -406,14 +413,11 @@
         name="root_backward",
     )(forward_sep, weights)
     solved = lax.all_to_all(solved, "grid", 0, 0, tiled=True)
-    solution_sep, picked = pl.pallas_call(
+    picked = pl.pallas_call(
         spread_kernel,
-        out_shape=(
-            jax.ShapeDtypeStruct((share_len, rhs_count), F32),
-            jax.ShapeDtypeStruct((tile_count, chunk_rows, LANES), BF16),
-        ),
+        out_shape=jax.ShapeDtypeStruct((tile_count, chunk_rows, LANES), BF16),
         in_specs=[VMEM, VMEM],
-        out_specs=(VMEM, VMEM),
+        out_specs=VMEM,
         scratch_shapes=[
             pltpu.VMEM((3, grid_count * own_pad, LANES), F32),
             pltpu.VMEM((rhs_count, LANES), F32),
@@ -424,21 +428,27 @@
         name="spread",
     )(solved, onehot)
     picked = lax.all_to_all(picked, "tile", 0, 0, tiled=True)
-    result = pl.pallas_call(
+    result, solution_sep = pl.pallas_call(
         functools.partial(backward_kernel, per_share),
-        out_shape=jax.ShapeDtypeStruct((rhs_count, local_len), BF16),
-        in_specs=[VMEM, VMEM, SMEM, VMEM, VMEM, VMEM],
-        out_specs=HBM,
+        out_shape=(
+            jax.ShapeDtypeStruct((rhs_count, local_len), BF16),
+            jax.ShapeDtypeStruct((share_len, rhs_count), F32),
+        ),
+        in_specs=[VMEM, VMEM, SMEM, VMEM, VMEM, VMEM, VMEM],
+        out_specs=(HBM, HBM),
         scratch_shapes=[
             pltpu.VMEM((tile_count, chunk_rows, LANES), F32),
             pltpu.VMEM((coupled_rows, 2 * LANES), F32),
             pltpu.VMEM((per_dev, rhs_count, block_len), BF16),
-            pltpu.SemaphoreType.DMA((per_dev,)),
+            pltpu.VMEM((3, grid_count * own_pad, LANES), F32),
+            pltpu.VMEM((rhs_count, LANES), F32),
+            pltpu.VMEM((share_len, rhs_count), F32),
+            pltpu.SemaphoreType.DMA((per_dev + 1,)),
         ],
         compiler_params=params(16 * MIB),
         cost_estimate=cost(2 * rhs_count * local_len * (block_len + coupled_rows), 5 << 20),
         name="backward",
-    )(picked, scales, live_rows, forward_flat, codes, diag_inv)
+    )(picked, scales, live_rows, forward_flat, codes, diag_inv, solved)
     return (result, solution_sep.T)
 
 

time: 106 us -> 105 us (level)
  no operation moved by 1% of the time
where the time goes in v7:
time: 105 us
  blocking collectives  68.8 us (66%)
  starting transfers between devices  12.6 us (12%)
  Pallas kernels  11.9 us (11%)
  waiting for transfers between devices  6.98 us (7%)
  local copies, waits for them, and re-layouts  2.95 us (3%)
  between operations  1.35 us (1%)
    all_to_all x1, blocking collectives, on_device(): picked = lax.all_to_all(picked, 'tile', 0, 0, tiled=True)  16.7 us
    all_to_all x1, blocking collectives, on_device(): arrived_sums = lax.all_to_all(sums, 'grid', 0, 0, tiled=True)  14.8 us
    all_to_all x1, blocking collectives, on_device(): lax.all_to_all(root_part, 'tile', 0, 0, tiled=True)  13.7 us
    all_to_all x1, blocking collectives, on_device(): forward_sep = lax.all_to_all(forward_sep, 'tile', 0, 0, tiled=True)  13.2 us
    all_to_all x1, starting transfers between devices, on_device(): arrived = lax.all_to_all(chunks, 'tile', 0, 0, tiled=True)  12.6 us
    all_to_all x1, blocking collectives, on_device(): solved = lax.all_to_all(solved, 'grid', 0, 0, tiled=True)  10.4 us
    all_to_all x1, waiting for transfers between devices, on_device(): arrived = lax.all_to_all(chunks, 'tile', 0, 0, tiled=True)  6.98 us
    pallas_call x1, Pallas kernels, on_device(): pl.pallas_call(functools.partial(forward_kernel, per_share, share_len), o...  4.56 us
  transfers between devices with their start and end apart: 1, of which 1 were waited for; matrix products, arithmetic and copies ran while one was open for 2% of the time, Pallas kernels for 2%

profile of v7, /device:TPU:64, one launch (start us, length us, event | category | flops | bytes accessed | tf_op | source)
XLA Modules:
  0.0 104.7 jit_solution(4165921197821336580)
XLA Ops:
  1.3 4.6 %forward.1 = (bf16[192,1536]{1,0:T(8,128)(2,1)}, bf16[32,32,128]{2,1,0:T(8,128)(2,1)}) custom-call(bf16[192,1536]{1,0:T(8,128)(2,1)} %rhs_hbm.1, bf16[3,512,512]{2,1,0:T(8,128)(2,1)} %diag.1, bf16[640,1536]{1,0:T(8,128)(2,1)} %codes.1, f32[5,128]{1,0:T(8,128)} %bitcast.3, s32[5,128]{1,0:T(8,128)} %bitcast.5, s32[1]{0:T(128)S(6)} %copy.15.live_ref), custom_call_target="tpu_custom_call" | custom-call | flops 679477248 | bytes 5242880 | tf_op jit(solution)/shard_map/forward/pallas_call | solution.py:330
  5.8 12.6 %all-to-all-start = ((bf16[32,32,128]{2,1,0:T(8,128)(2,1)}), bf16[32,32,128]{2,1,0:T(8,128)(2,1)S(1)}, u32[]{:S(2)}, u32[]{:S(2)}) async-start(bf16[32,32,128]{2,1,0:T(8,128)(2,1)} %get-tuple-element.11), calls=%async_computation | async-start | bytes 524288 | tf_op jit(solution)/shard_map/all_to_all | solution.py:352
  18.5 0.8 constant_dynamic-slice_fusion
  19.3 0.1 copy.13
  19.4 0.1 copy.14
  19.4 0.9 constant_dynamic-slice_fusion.1
  20.3 0.1 copy.12
  20.4 1.0 copy-done.3
  21.4 2.3 %weights.1.weights_ref = bf16[256,4096]{1,0:T(8,128)(2,1)S(1)} custom-call(bf16[80,2560]{1,0:T(8,128)(2,1)S(1)} %copy-done.3), custom_call_target="tpu_custom_call" | custom-call | flops 3276800 | bytes 3145728 | tf_op jit(solution)/shard_map/weights/pallas_call | solution.py:354
  23.7 0.1 fusion.4.right_ref
  23.7 7.0 %all-to-all-done.chunks_ref = bf16[32,32,128]{2,1,0:T(8,128)(2,1)S(1)} async-done(((bf16[32,32,128]{2,1,0:T(8,128)(2,1)}), bf16[32,32,128]{2,1,0:T(8,128)(2,1)S(1)}, u32[]{:S(2)}, u32[]{:S(2)}) %all-to-all-start) | async-done | bytes 262176 | tf_op jit(solution)/shard_map/all_to_all | solution.py:352
  30.7 0.9 gather_sum.1
  31.6 14.8 %all_to_all.30.sums_ref = f32[16,8,128]{2,1,0:T(8,128)S(1)} all-to-all(f32[16,8,128]{2,1,0:T(8,128)S(1)} %get-tuple-element.13), channel_id=1, replica_groups=mesh['grid'=16,'tile'=32] {'grid'}, dimensions={0} | all-to-all | bytes 131072 | tf_op jit(solution)/shard_map/all_to_all | solution.py:387
  46.4 0.5 root_forward.1
  46.9 13.7 %all_to_all.31.parts_ref = bf16[32,8,128]{2,1,0:T(8,128)(2,1)S(1)} all-to-all(bf16[32,8,128]{2,1,0:T(8,128)(2,1)S(1)} %root_forward.1), channel_id=1, replica_groups=mesh['grid'=16,'tile'=32] {'tile'}, dimensions={0} | all-to-all | bytes 131072 | tf_op jit(solution)/shard_map/all_to_all | solution.py:404
  60.6 13.2 %all_to_all.32.forward_ref = bf16[32,8,128]{2,1,0:T(8,128)(2,1)S(1)} all-to-all(bf16[32,8,128]{2,1,0:T(8,128)(2,1)S(1)} %root_middle.1), channel_id=1, replica_groups=mesh['grid'=16,'tile'=32] {'tile'}, dimensions={0} | all-to-all | bytes 131072 | tf_op jit(solution)/shard_map/all_to_all | solution.py:405
  73.8 0.8 root_backward.1
  74.6 10.4 %all_to_all.33.solved_ref = bf16[16,8,128]{2,1,0:T(8,128)(2,1)S(1)} all-to-all(bf16[16,8,128]{2,1,0:T(8,128)(2,1)S(1)} %root_backward.1), channel_id=1, replica_groups=mesh['grid'=16,'tile'=32] {'grid'}, dimensions={0} | all-to-all | bytes 65536 | tf_op jit(solution)/shard_map/all_to_all | solution.py:415
  85.0 0.5 spread.1
  85.5 16.7 %all_to_all.34.chunks_ref = bf16[32,32,128]{2,1,0:T(8,128)(2,1)S(1)} all-to-all(bf16[32,32,128]{2,1,0:T(8,128)(2,1)S(1)} %spread.1), channel_id=1, replica_groups=mesh['grid'=16,'tile'=32] {'tile'}, dimensions={0} | all-to-all | bytes 524288 | tf_op jit(solution)/shard_map/all_to_all | solution.py:430
  102.2 0.0 copy-done.4
  102.2 0.0 copy-done
  102.2 0.0 copy-done.1
  102.2 2.5 %backward.1 = (bf16[192,1536]{1,0:T(8,128)(2,1)}, f32[80,192]{1,0:T(8,128)}) custom-call(bf16[32,32,128]{2,1,0:T(8,128)(2,1)S(1)} %all_to_all.34.chunks_ref, f32[5,128]{1,0:T(8,128)S(1)} %bitcast.4, s32[1]{0:T(128)S(6)} %copy.15.live_ref, bf16[192,1536]{1,0:T(8,128)(2,1)S(1)} %copy-done.2, bf16[640,1536]{1,0:T(8,128)(2,1)S(1)} %copy-done, ...), custom_call_target="tpu_custom_call" | custom-call | flops 679477248 | bytes 5242880 | tf_op jit(solution)/shard_map/backward/pallas_call | solution.py:431
  (7 shorter events, 0.1 us)
Async XLA Ops:
  5.8 24.9 %all-to-all-start = ((bf16[32,32,128]{2,1,0:T(8,128)(2,1)}), bf16[32,32,128]{2,1,0:T(8,128)(2,1)S(1)}, u32[]{:S(2)}, u32[]{:S(2)}) async-start(bf16[32,32,128]{2,1,0:T(8,128)(2,1)} %get-tuple-element.11), calls=%async_computation | async-start | bytes 524288 | tf_op jit(solution)/shard_map/all_to_all | solution.py:352
  20.4 1.0 copy-start.3
  46.9 55.3 %copy-start.4 = (f32[640]{0:T(1024)S(1)}, f32[640]{0:T(1024)}, u32[]{:S(2)}) copy-start(f32[640]{0:T(1024)} %param.11) | copy-start | bytes 7684
  60.6 41.6 %copy-start.2 = (bf16[192,1536]{1,0:T(8,128)(2,1)S(1)}, bf16[192,1536]{1,0:T(8,128)(2,1)}, u32[]{:S(2)}) copy-start(bf16[192,1536]{1,0:T(8,128)(2,1)} %get-tuple-element.17.forward_ref) | copy-start | bytes 1769476
  73.8 28.4 %copy-start = (bf16[640,1536]{1,0:T(8,128)(2,1)S(1)}, bf16[640,1536]{1,0:T(8,128)(2,1)}, u32[]{:S(2)}) copy-start(bf16[640,1536]{1,0:T(8,128)(2,1)} %codes.1) | copy-start | bytes 5898244
  73.8 28.4 %copy-start.1 = (bf16[3,512,512]{2,1,0:T(8,128)(2,1)S(1)}, bf16[3,512,512]{2,1,0:T(8,128)(2,1)}, u32[]{:S(2)}) copy-start(bf16[3,512,512]{2,1,0:T(8,128)(2,1)} %diag.1) | copy-start | bytes 4718596
